TPU v7x, 32 devices: a whole 2x2x4 slice. The times are simulated.
32 devices in a mesh: row: 4 (over y, core), col: 8 (over z, x).
Axes of the slice: x: 2, y: 2, z: 4, core: 2. Of those that a mesh axis runs over, the one named last changes fastest.
Arguments:
- patches: float32 [32, 64, 2, 128, 128], P('row', 'col'), may hold values from -6 to 6
- right_offset: int32 [32, 64], P('row', 'col'), may hold values from 57 to 112, as said below
- right_width: int32 [32, 64], P('row', 'col'), may hold values from 16 to 64
- down_offset: int32 [32, 64], P('row', 'col'), may hold values from 57 to 112, as said below
- down_width: int32 [32, 64], P('row', 'col'), may hold values from 16 to 64
Outputs:
- blended: float32 [32, 64, 2, 128, 128], P('row', 'col')
- phases: float32 [2, 32, 64], P(None, 'row', 'col')
Inputs may be any that keep to these rules, and one draw needn't show every extreme that they name: right_offset + right_width lies above 120 and at most 128. down_offset + down_width lies above 120 and at most 128.
All inputs are finite; a program needn't handle non-finite values.
Results may differ from a plain program's by a relative error of at most 0.0003.
Values sent between devices are 32-bit elements; how exact they have to be, the bound alone decides.
A program may use at most 128 MiB of HBM per device.

v0:
```python
import functools

import jax
import jax.numpy as jnp
from jax import lax
from jax.experimental import pallas as pl
from jax.experimental.pallas import tpu as pltpu
from jax.sharding import PartitionSpec as P

ITERS = 2
PAD = 64
eps_norm = 1.0
highest = lax.Precision.HIGHEST
MESH = pl.DeviceIdType.MESH
f32 = jnp.float32


def fold_rows(x):
    return jnp.sum(x, axis=0, keepdims=True)


def doubling(pos, n, at):
    if n == 1:
        return []
    rounds = [[at(-1) + (pos > 0, pos < n - 1)]]
    known = 1
    while known < n - 1:
        rounds.append([
            at(-known) + (pos >= known, pos < n - known),
            at(known) + (pos < n - known, pos >= known),
        ])
        known *= 2
    return rounds


def n_rounds(n):
    return len(doubling(0, n, lambda k: (0, 0)))


def sync_kernel(
    dims, patches, ro_in, rw_in, do_in, dw_in, pv, east_recv, south_recv, phase_out,
    epack, acc, send_buf, recv, fields, ro, rw, do, dw,
    col_sem, rest_sem, e_send, e_recv, s_send, s_recv, g_send, g_recv, table_sem, round_sem,
):
    R, C, S, nr, nc = dims
    H, ndev = S // 2, nr * nc
    lo = H - 8
    my_row, my_col = lax.axis_index("row"), lax.axis_index("col")
    me = my_row * nc + my_col

    turn_rows = [lax.rem(my_row + k, nr) for k in range(nr)]
    turn_cols = [lax.rem(my_col + k, nc) for k in range(nc)]
    others = [
        (turn_rows[a], turn_cols[b]) for a in range(nr) for b in range(nc) if a or b
    ]
    barrier = pltpu.get_barrier_semaphore()

    def signal(sem, row, col, there):
        @pl.when(there)
        def _():
            pl.semaphore_signal(sem, inc=1, device_id=(row, col), device_id_type=MESH)

    def await_all(sem, *due):
        amount = sum(one.astype(jnp.int32) for one in due)

        @pl.when(amount > 0)
        def _():
            pl.semaphore_wait(sem, amount)

    steps = doubling(my_row, nr, lambda k: (my_row + k, my_col))
    steps += doubling(my_col, nc, lambda k: (my_row, my_col + k))

    def tell(k):
        for row, col, there, _ in steps[k]:
            signal(round_sem.at[k], row, col, there)

    def hear(k):
        await_all(round_sem.at[k], *(here for _, _, _, here in steps[k]))

    def spread(k):
        if k < len(steps):
            hear(k)
            if k + 1 < len(steps):
                tell(k + 1)

    cols = [
        pltpu.make_async_copy(
            patches.at[pl.ds(i * C * 2 * S, 2 * S)],
            pv.at[pl.ds(PAD + i * C * 2 * S, 2 * S)],
            col_sem.at[i],
        )
        for i in range(R)
    ]
    rests = [
        pltpu.make_async_copy(
            patches.at[pl.ds((i * C + 1) * 2 * S, (C - 1) * 2 * S)],
            pv.at[pl.ds(PAD + (i * C + 1) * 2 * S, (C - 1) * 2 * S)],
            rest_sem.at[i],
        )
        for i in range(R)
    ]
    tables = [
        pltpu.make_async_copy(here, there, table_sem.at[k])
        for k, (here, there) in enumerate(zip((ro_in, rw_in, do_in, dw_in), (ro, rw, do, dw)))
    ]
    for copy in cols:
        copy.start()
    signal(barrier, my_row + 1, my_col, my_row < nr - 1)
    signal(barrier, my_row, my_col + 1, my_col < nc - 1)
    for copy in tables:
        copy.start()
    for copy in rests:
        copy.start()
    lane = lax.broadcasted_iota(jnp.int32, (S, S), 1)

    def pack(i):
        base = PAD + i * C * 2 * S
        cols[i].wait()
        re = pv[pl.ds(base, S), :]
        im = pv[pl.ds(base + S, S), :]
        epack[pl.ds(i * S, S), :] = jnp.where(lane < H, re, pltpu.roll(im, H, 1))

    def south_copy(k, row):
        return pltpu.make_async_remote_copy(
            src_ref=patches.at[pl.ds(k * S, H)],
            dst_ref=south_recv.at[pl.ds(PAD + k * H, H)],
            send_sem=s_send.at[k],
            recv_sem=s_recv.at[k],
            device_id=(row, my_col),
            device_id_type=MESH,
        )

    def east_copy(k, col):
        return pltpu.make_async_remote_copy(
            src_ref=epack.at[pl.ds(k * S, S)],
            dst_ref=east_recv.at[pl.ds(k * S, S)],
            send_sem=e_send.at[k],
            recv_sem=e_recv.at[k],
            device_id=(my_row, col),
            device_id_type=MESH,
        )

    def send_east(i):
        @pl.when(my_col > 0)
        def _():
            east_copy(i, my_col - 1).start()

    for i in range(2):
        pack(i)
    await_all(barrier, my_row > 0, my_col > 0)
    for i in range(2):
        send_east(i)

    @pl.when(my_row > 0)
    def _():
        for k in range(2 * C):
            south_copy(k, my_row - 1).start()

    if steps:
        tell(0)
    for i in range(2, R):
        pack(i)
        send_east(i)
    acc[...] = jnp.zeros_like(acc)
    for copy in tables:
        copy.wait()
    for copy in rests:
        copy.wait()

    lane1 = lax.broadcasted_iota(jnp.int32, (1, S), 1)
    row8 = lax.broadcasted_iota(jnp.int32, (8, S), 0)

    def put(plane, p, re, im, width):
        scale = 1.0 / jnp.sqrt(jnp.full((1, S), S * width, jnp.int32).astype(f32))
        acc[pl.ds(plane * R * C + p, 1), :] = fold_rows(re) * scale
        acc[pl.ds((plane + 1) * R * C + p, 1), :] = fold_rows(im) * scale

    def gathered(pieces):
        re, im = None, None
        for a_re, a_im, b_re, b_im in pieces:
            u, v = a_re * b_re + a_im * b_im, a_re * b_im - a_im * b_re
            re, im = (u, v) if re is None else (re + u, im + v)
        return re, im

    def east_store(i, j, load_b):
        p = i * C + j
        o, w = ro[i, j], rw[i, j]
        base = PAD + p * 2 * S
        re, im = gathered(
            (pv[pl.ds(pl.multiple_of(base + q, 8), 8), :],
             pv[pl.ds(pl.multiple_of(base + S + q, 8), 8), :]) + load_b(q, o)
            for q in range(0, S, 8)
        )
        keep = (lane1 >= o) & (lane1 < o + w)
        put(0, p, jnp.where(keep, re, 0.0), jnp.where(keep, im, 0.0), w)

    def east_inner(i, carry):
        for j in range(C - 1):
            base = PAD + (i * C + j + 1) * 2 * S

            def load_b(q, o):
                return (
                    pltpu.roll(pv[pl.ds(pl.multiple_of(base + q, 8), 8), :], o, 1),
                    pltpu.roll(pv[pl.ds(pl.multiple_of(base + S + q, 8), 8), :], o, 1),
                )

            east_store(i, j, load_b)
        return carry

    def south_store(i, j, ref, start, gap):
        p = i * C + j
        o, w = do[i, j], dw[i, j]
        base = PAD + p * 2 * S

        def piece(q):
            keep = row8 >= o - q if q < S - 8 else row8 < o + w - q
            b_re = ref[pl.ds(start + (q - o), 8), :]
            b_im = ref[pl.ds(start + gap + (q - o), 8), :]
            return (
                pv[pl.ds(pl.multiple_of(base + q, 8), 8), :],
                pv[pl.ds(pl.multiple_of(base + S + q, 8), 8), :],
                jnp.where(keep, b_re, 0.0),
                jnp.where(keep, b_im, 0.0),
            )

        re, im = gathered(piece(q) for q in range(lo, S, 8))
        put(2, p, re, im, w)

    def south_inner(i, carry):
        for j in range(C):
            south_store(i, j, pv, PAD + ((i + 1) * C + j) * 2 * S, S)
        return carry

    spread(0)
    lax.fori_loop(0, R // 2, east_inner, 0)
    spread(1)
    lax.fori_loop(R // 2, R, east_inner, 0)
    spread(2)
    lax.fori_loop(0, R // 2, south_inner, 0)
    spread(3)
    lax.fori_loop(R // 2, R - 1, south_inner, 0)
    spread(4)

    @pl.when(my_row < nr - 1)
    def _():
        for k in range(2 * C):
            south_copy(k, my_row).wait_recv()

    @pl.when(my_row == nr - 1)
    def _():
        south_recv[...] = jnp.zeros_like(south_recv)

    for j in range(C):
        south_store(R - 1, j, south_recv, PAD + j * 2 * H, H)

    for k in range(5, len(steps)):
        spread(k)

    @pl.when(my_col == nc - 1)
    def _():
        east_recv[...] = jnp.zeros_like(east_recv)

    for i in range(R):

        @pl.when(my_col < nc - 1)
        def _():
            east_copy(i, my_col).wait_recv()

        def load_b(q, o):
            both = east_recv[pl.ds(i * S + q, 8), :]
            return pltpu.roll(both, o, 1), pltpu.roll(both, lax.rem(o + H, S), 1)

        east_store(i, C - 1, load_b)

    sums = lax.dot_general(
        jnp.ones((8, S), f32), acc[...], (((1,), (1,)), ((), ())),
        precision=highest, preferred_element_type=f32,
    )
    mine = jnp.concatenate([sums[0:1, :S], sums[0:1, S:]], axis=0)
    send_buf[...] = mine
    recv[me] = mine

    def index(d):
        return d[0] * nc + d[1]

    def gather_copy(target, source):
        return pltpu.make_async_remote_copy(
            src_ref=send_buf,
            dst_ref=recv.at[index(source)],
            send_sem=g_send.at[index(target)],
            recv_sem=g_recv.at[index(source)],
            device_id=target,
            device_id_type=MESH,
        )

    for other in others:
        gather_copy(other, (my_row, my_col)).start()
    for other in others:
        gather_copy(other, other).wait_recv()

    got = recv[...]
    east, south = got[:, 0, :], got[:, 1, :]
    field = lax.broadcasted_iota(jnp.int32, (ndev, S), 0)
    slot = lax.broadcasted_iota(jnp.int32, (ndev, S), 1)
    valid = slot < R * C
    j_of, i_of = slot % C, (slot // C) % R
    dc, dr = field % nc, field // nc

    def roll(x, by, axis):
        return pltpu.roll(x, by % x.shape[axis], axis)

    def from_east(x):
        far = roll(roll(x, -1, 0), C - 1, 1)
        far = jnp.where(dc < nc - 1, far, 0.0)
        return jnp.where(j_of < C - 1, roll(x, -1, 1), far)

    def from_west(x):
        far = roll(roll(x, 1, 0), 1 - C, 1)
        far = jnp.where(dc > 0, far, 0.0)
        return jnp.where(j_of > 0, roll(x, 1, 1), far)

    def from_south(x):
        far = roll(roll(x, -nc, 0), (R - 1) * C, 1)
        far = jnp.where(dr < nr - 1, far, 0.0)
        return jnp.where(i_of < R - 1, roll(x, -C, 1), far)

    def from_north(x):
        far = roll(roll(x, nc, 0), -(R - 1) * C, 1)
        far = jnp.where(dr > 0, far, 0.0)
        return jnp.where(i_of > 0, roll(x, C, 1), far)

    ce = (jnp.where(valid, east, 0.0), jnp.where(valid, roll(east, -R * C, 1), 0.0))
    cs = (jnp.where(valid, south, 0.0), jnp.where(valid, roll(south, -R * C, 1), 0.0))
    cw = tuple(from_west(x) for x in ce)
    cn = tuple(from_north(x) for x in cs)
    count = float(ndev * R * C)

    def times(a, b):
        return (a[0] * b[0] - a[1] * b[1], a[0] * b[1] + a[1] * b[0])

    def conj_times(a, b):
        return (a[0] * b[0] + a[1] * b[1], a[0] * b[1] - a[1] * b[0])

    now = (jnp.ones((ndev, S), f32), jnp.zeros((ndev, S), f32))
    for step in range(ITERS):
        terms = (
            times(ce, tuple(from_east(x) for x in now)),
            times(cs, tuple(from_south(x) for x in now)),
            conj_times(cw, tuple(from_west(x) for x in now)),
            conj_times(cn, tuple(from_north(x) for x in now)),
        )
        image = tuple(
            jnp.where(valid, terms[0][q] + terms[1][q] + terms[2][q] + terms[3][q], 0.0)
            for q in range(2)
        )
        total = jnp.sum(image[0] * image[0] + image[1] * image[1], axis=0, keepdims=True)
        total = jnp.sum(total, axis=1, keepdims=True)
        factor = 1.0 / jnp.sqrt(total / count + eps_norm)
        now = (image[0] * factor, image[1] * factor)
    outs = now + tuple(from_east(x) for x in now) + tuple(from_south(x) for x in now)
    for q in range(6):
        fields[q] = outs[q]
    for q in range(6):
        phase_out[q : q + 1, :] = fields[q, pl.ds(me, 1), :]
    phase_out[6:8, :] = jnp.zeros((2, S), f32)

    for other in others:
        gather_copy(other, (my_row, my_col)).wait_send()

    @pl.when(my_col > 0)
    def _():
        for k in range(R):
            east_copy(k, my_col - 1).wait_send()

    @pl.when(my_row > 0)
    def _():
        for k in range(2 * C):
            south_copy(k, my_row - 1).wait_send()


def blend_kernel(
    dims, pv, ev, sv, ro, rw, do, dw, g, out, phases, ov, out_sem,
):
    R, C, S, nr, nc = dims
    H = S // 2
    lo = H - 8
    row_size = C * 2 * S
    last_col = lax.axis_index("col") == nc - 1
    last_row = lax.axis_index("row") == nr - 1

    def save(i):
        return pltpu.make_async_copy(
            ov.at[pl.ds(i * row_size, row_size)],
            out.at[pl.ds(i * row_size, row_size)],
            out_sem.at[i],
        )

    lane = lax.broadcasted_iota(jnp.int32, (1, S), 1)
    row8 = lax.broadcasted_iota(jnp.int32, (8, S), 0)

    def at(ref, row):
        return ref[pl.ds(pl.multiple_of(row, 8), 8), :]

    def place(i, j, east, ref, start, gap):
        p = i * C + j
        oe, we, os, ws = ro[i, j], rw[i, j], do[i, j], dw[i, j]
        g_re, g_im = g[0, p], g[1, p]
        ge_re, ge_im, gs_re, gs_im = g[2, p], g[3, p], g[4, p], g[5, p]
        phases[0, i, j] = g_re
        phases[1, i, j] = g_im
        base = PAD + p * 2 * S
        to = p * 2 * S
        keep_e = (lane >= oe) & (lane < oe + we)
        live_e = keep_e & jnp.logical_not((j == C - 1) & last_col)
        half = jnp.where(live_e, f32(0.5), f32(1.0))
        third = jnp.where(live_e, f32(1.0 / 3.0), f32(0.5))
        down = jnp.logical_not((i == R - 1) & last_row)
        third = jnp.where(jnp.full((1, S), down), third, half)
        half, third = jnp.broadcast_to(half, (8, S)), jnp.broadcast_to(third, (8, S))
        e_re = jnp.broadcast_to(jnp.where(keep_e, ge_re, 0.0), (8, S))
        e_im = jnp.broadcast_to(jnp.where(keep_e, ge_im, 0.0), (8, S))
        h_re, h_im, x_re, x_im = g_re * half, g_im * half, e_re * half, e_im * half
        for q in range(0, S, 8):
            a_re, a_im = at(pv, base + q), at(pv, base + S + q)
            b_re, b_im = east(q, oe)
            if q < lo:
                n_re = (h_re * a_re - h_im * a_im) + (x_re * b_re - x_im * b_im)
                n_im = (h_re * a_im + h_im * a_re) + (x_re * b_im + x_im * b_re)
            else:
                keep = row8 >= os - q if q < S - 8 else row8 < os + ws - q
                s_re = ref[pl.ds(start + (q - os), 8), :]
                s_im = ref[pl.ds(start + gap + (q - os), 8), :]
                n_re = (g_re * a_re - g_im * a_im) + (e_re * b_re - e_im * b_im)
                n_im = (g_re * a_im + g_im * a_re) + (e_re * b_im + e_im * b_re)
                inv = jnp.where(keep, third, half)
                n_re = (n_re + jnp.where(keep, gs_re * s_re - gs_im * s_im, 0.0)) * inv
                n_im = (n_im + jnp.where(keep, gs_re * s_im + gs_im * s_re, 0.0)) * inv
            ov[pl.ds(pl.multiple_of(to + q, 8), 8), :] = n_re
            ov[pl.ds(pl.multiple_of(to + S + q, 8), 8), :] = n_im

    def east_of(i, j):
        base = PAD + (i * C + j + 1) * 2 * S

        def east(q, o):
            return pltpu.roll(at(pv, base + q), o, 1), pltpu.roll(at(pv, base + S + q), o, 1)

        return east

    def east_rim(i):
        def east(q, o):
            both = at(ev, i * S + q)
            return pltpu.roll(both, o, 1), pltpu.roll(both, lax.rem(o + H, S), 1)

        return east

    def south_of(i, j):
        return pv, PAD + ((i + 1) * C + j) * 2 * S, S

    def south_rim(j):
        return sv, PAD + j * 2 * H, H

    def rows(i, carry):
        for j in range(C):
            place(i, j, east_of(i, j) if j < C - 1 else east_rim(i), *south_of(i, j))
        save(i).start()
        return carry

    lax.fori_loop(0, R - 1, rows, 0)
    for j in range(C):
        place(R - 1, j, east_of(R - 1, j) if j < C - 1 else east_rim(R - 1), *south_rim(j))
    save(R - 1).start()
    for i in range(R):
        save(i).wait()


def local(nr, nc, patches, right_offset, right_width, down_offset, down_width):
    R, C, _, S, _ = patches.shape
    H, ndev = S // 2, nr * nc
    dims = (R, C, S, nr, nc)
    flat = patches.reshape(R * C * 2 * S, S)
    anyspec = pl.BlockSpec(memory_space=pl.ANY)
    smem = pl.BlockSpec(memory_space=pltpu.SMEM)
    vmem = pl.BlockSpec(memory_space=pltpu.VMEM)
    dma = pltpu.SemaphoreType.DMA
    tables = (right_offset, right_width, down_offset, down_width)
    pv, east_halo, south_halo, phase = pl.pallas_call(
        functools.partial(sync_kernel, dims),
        out_shape=(
            pltpu.VMEM((PAD + R * C * 2 * S, S), f32),
            pltpu.VMEM((R * S, S), f32),
            pltpu.VMEM((2 * PAD + 2 * C * H, S), f32),
            jax.ShapeDtypeStruct((8, S), f32),
        ),
        in_specs=[pl.BlockSpec(memory_space=pltpu.HBM)] * 5,
        out_specs=(vmem,) * 4,
        scratch_shapes=[
            pltpu.VMEM((R * S, S), f32),
            pltpu.VMEM((4 * R * C, S), f32),
            pltpu.VMEM((2, S), f32),
            pltpu.VMEM((ndev, 2, S), f32),
            pltpu.VMEM((6, ndev, S), f32),
        ] + [pltpu.SMEM((R, C), jnp.int32)] * 4 + [
            dma((R,)), dma((R,)),
            dma((R,)), dma((R,)),
            dma((2 * C,)), dma((2 * C,)),
            dma((ndev,)), dma((ndev,)),
            dma((4,)),
            pltpu.SemaphoreType.REGULAR((n_rounds(nr) + n_rounds(nc),)),
        ],
        compiler_params=pltpu.CompilerParams(
            collective_id=0, has_side_effects=True, vmem_limit_bytes=16 << 20
        ),
        name="sync_patches",
    )(*(pltpu.with_memory_space_constraint(x, pltpu.HBM) for x in (flat, *tables)))
    blended, phases = pl.pallas_call(
        functools.partial(blend_kernel, dims),
        out_shape=(
            jax.ShapeDtypeStruct((R * C * 2 * S, S), f32),
            jax.ShapeDtypeStruct((2, R, C), f32),
        ),
        in_specs=[vmem] * 3 + [smem] * 5,
        out_specs=(anyspec, smem),
        scratch_shapes=[
            pltpu.VMEM((R * C * 2 * S, S), f32),
            dma((R,)),
        ],
        compiler_params=pltpu.CompilerParams(vmem_limit_bytes=24 << 20),
        name="blend_patches",
    )(pv, east_halo, south_halo, *tables, phase)
    return blended.reshape(patches.shape), phases


def solution(mesh):
    return jax.shard_map(
        functools.partial(local, mesh.shape["row"], mesh.shape["col"]),
        mesh=mesh,
        in_specs=(P("row", "col", None, None, None),) + (P("row", "col"),) * 4,
        out_specs=(P("row", "col", None, None, None), P(None, "row", "col")),
        check_vma=False,
    )
```

profile of v0, /device:TPU:0, one launch (start us, length us, event | category | flops | bytes accessed | tf_op | source)
XLA Modules:
  0.0 31.5 jit_solution(1384693078297144399)
XLA Ops:
  0.6 0.0 copy-start.3
  0.6 0.0 copy-start.2
  0.7 0.0 copy-start.1
  0.7 0.0 copy-start
  0.7 24.6 %sync_patches.1 = (f32[16448,128]{1,0:T(8,128)S(1)}, f32[1024,128]{1,0:T(8,128)S(1)}, f32[1152,128]{1,0:T(8,128)S(1)}, f32[8,128]{1,0:T(8,128)S(1)}) custom-call(f32[16384,128]{1,0:T(8,128)} %bitcast.2, s32[8,8]{1,0:T(8,128)} %ro.1, s32[8,8]{1,0:T(8,128)} %rw.1, s32[8,8]{1,0:T(8,128)} %do.1, s32[8,8]{1,0:T(8,128)} %dw.1), custom_call_target="tpu_custom_call" | custom-call | tf_op jit(solution)/shard_map/sync_patches/pallas_call | solution.py:486
  25.2 0.0 copy-done.3
  25.3 0.0 copy-done.2
  25.3 0.0 copy-done.1
  25.3 0.0 copy-done
  25.3 6.2 %blend_patches.1 = (f32[16384,128]{1,0:T(8,128)}, f32[2,8,8]{2,1,0:T(8,128)}) custom-call(f32[16448,128]{1,0:T(8,128)S(1)} %get-tuple-element.8.pv, f32[1024,128]{1,0:T(8,128)S(1)} %get-tuple-element.9.ev, f32[1152,128]{1,0:T(8,128)S(1)} %get-tuple-element.10.sv, s32[8,8]{1,0:T(8,128)S(1)} %copy-done, s32[8,8]{1,0:T(8,128)S(1)} %copy-done.1, ...), custom_call_target="tpu_custom_call" | custom-call | tf_op jit(solution)/shard_map/blend_patches/pallas_call | solution.py:515
Async XLA Ops:
  0.6 24.6 %copy-start.3 = (s32[8,8]{1,0:T(8,128)S(1)}, s32[8,8]{1,0:T(8,128)}, u32[]{:S(2)}) copy-start(s32[8,8]{1,0:T(8,128)} %dw.1) | copy-start | bytes 772
  0.6 24.6 %copy-start.2 = (s32[8,8]{1,0:T(8,128)S(1)}, s32[8,8]{1,0:T(8,128)}, u32[]{:S(2)}) copy-start(s32[8,8]{1,0:T(8,128)} %do.1) | copy-start | bytes 772
  0.7 24.6 %copy-start.1 = (s32[8,8]{1,0:T(8,128)S(1)}, s32[8,8]{1,0:T(8,128)}, u32[]{:S(2)}) copy-start(s32[8,8]{1,0:T(8,128)} %rw.1) | copy-start | bytes 772
  0.7 24.6 %copy-start = (s32[8,8]{1,0:T(8,128)S(1)}, s32[8,8]{1,0:T(8,128)}, u32[]{:S(2)}) copy-start(s32[8,8]{1,0:T(8,128)} %ro.1) | copy-start | bytes 772
where the time goes:
time: 31.7 us; the launch traced here: 31.5 us
  Pallas kernels  30.8 us (97%)
  between operations  0.7 us (2%)
    pallas_call x1, Pallas kernels, local(): pl.pallas_call(functools.partial(sync_kernel, dims), out_shape=(pltpu.VME...  24.6 us
    pallas_call x1, Pallas kernels, local(): pl.pallas_call(functools.partial(blend_kernel, dims), out_shape=(jax.Shap...  6.23 us

commit v1 on v0

--- a/solution.py
+++ b/solution.py
@@ -38,15 +38,18 @@
 
 
 def sync_kernel(
-    dims, patches, ro_in, rw_in, do_in, dw_in, pv, east_recv, south_recv, phase_out,
+    dims, patches, ro_in, rw_in, do_in, dw_in, aw, ew, sw, factors, phase_out,
+    pv, east_recv, south_recv,
     epack, acc, send_buf, recv, fields, ro, rw, do, dw,
     col_sem, rest_sem, e_send, e_recv, s_send, s_recv, g_send, g_recv, table_sem, round_sem,
 ):
     R, C, S, nr, nc = dims
     H, ndev = S // 2, nr * nc
     lo = H - 8
+    T = S - lo
     my_row, my_col = lax.axis_index("row"), lax.axis_index("col")
     me = my_row * nc + my_col
+    last_col, last_row = my_col == nc - 1, my_row == nr - 1
 
     turn_rows = [lax.rem(my_row + k, nr) for k in range(nr)]
     turn_cols = [lax.rem(my_col + k, nc) for k in range(nc)]
@@ -74,12 +77,9 @@
         for row, col, there, _ in steps[k]:
             signal(round_sem.at[k], row, col, there)
 
-    def hear(k):
-        await_all(round_sem.at[k], *(here for _, _, _, here in steps[k]))
-
     def spread(k):
         if k < len(steps):
-            hear(k)
+            await_all(round_sem.at[k], *(here for _, _, _, here in steps[k]))
             if k + 1 < len(steps):
                 tell(k + 1)
 
@@ -170,6 +170,12 @@
     lane1 = lax.broadcasted_iota(jnp.int32, (1, S), 1)
     row8 = lax.broadcasted_iota(jnp.int32, (8, S), 0)
 
+    def at(ref, row):
+        return ref[pl.ds(pl.multiple_of(row, 8), 8), :]
+
+    def put_at(ref, row, value):
+        ref[pl.ds(pl.multiple_of(row, 8), 8), :] = value
+
     def put(plane, p, re, im, width):
         scale = 1.0 / jnp.sqrt(jnp.full((1, S), S * width, jnp.int32).astype(f32))
         acc[pl.ds(plane * R * C + p, 1), :] = fold_rows(re) * scale
@@ -182,53 +188,91 @@
             re, im = (u, v) if re is None else (re + u, im + v)
         return re, im
 
-    def east_store(i, j, load_b):
+    def weights(i, j, within):
+        o, w = ro[i, j], rw[i, j]
+        keep = (lane1 >= o) & (lane1 < o + w)
+        live = keep if j < C - 1 else keep & jnp.logical_not(last_col)
+        half = jnp.where(live, f32(0.5), f32(1.0))
+        third = jnp.where(live, f32(1.0 / 3.0), f32(0.5))
+        down = jnp.logical_not((i == R - 1) & last_row)
+        third = jnp.where(jnp.full((1, S), down), third, half)
+        if within:
+            half, third = jnp.where(keep, half, 0.0), jnp.where(keep, third, 0.0)
+        return jnp.broadcast_to(half, (8, S)), jnp.broadcast_to(third, (8, S))
+
+    def reached(i, j, q):
+        o, w = do[i, j], dw[i, j]
+        return row8 >= o - q if q < S - 8 else row8 < o + w - q
+
+    def weight_at(i, j, q, half, third):
+        return half if q < lo else jnp.where(reached(i, j, q), third, half)
+
+    def rows_of(p):
+        return PAD + p * 2 * S
+
+    def east_of(i, j):
+        base = rows_of(i * C + j + 1)
+
+        def load(q, o):
+            return pltpu.roll(at(pv, base + q), o, 1), pltpu.roll(at(pv, base + S + q), o, 1)
+
+        return load
+
+    def east_rim(i):
+        def load(q, o):
+            both = at(east_recv, i * S + q)
+            return pltpu.roll(both, o, 1), pltpu.roll(both, lax.rem(o + H, S), 1)
+
+        return load
+
+    def place_east(i, j, q, b, half, third):
+        to = (i * C + j) * 2 * S + q
+        weight = weight_at(i, j, q, half, third)
+        put_at(ew, to, b[0] * weight)
+        put_at(ew, to + S, b[1] * weight)
+
+    def east_store(i, j, load, place):
         p = i * C + j
         o, w = ro[i, j], rw[i, j]
-        base = PAD + p * 2 * S
-        re, im = gathered(
-            (pv[pl.ds(pl.multiple_of(base + q, 8), 8), :],
-             pv[pl.ds(pl.multiple_of(base + S + q, 8), 8), :]) + load_b(q, o)
-            for q in range(0, S, 8)
-        )
+        base = rows_of(p)
+        half, third = weights(i, j, True)
+
+        def piece(q):
+            b = load(q, o)
+            if place:
+                place_east(i, j, q, b, half, third)
+            return (at(pv, base + q), at(pv, base + S + q)) + b
+
+        re, im = gathered(piece(q) for q in range(0, S, 8))
         keep = (lane1 >= o) & (lane1 < o + w)
         put(0, p, jnp.where(keep, re, 0.0), jnp.where(keep, im, 0.0), w)
 
     def east_inner(i, carry):
         for j in range(C - 1):
-            base = PAD + (i * C + j + 1) * 2 * S
-
-            def load_b(q, o):
-                return (
-                    pltpu.roll(pv[pl.ds(pl.multiple_of(base + q, 8), 8), :], o, 1),
-                    pltpu.roll(pv[pl.ds(pl.multiple_of(base + S + q, 8), 8), :], o, 1),
-                )
-
-            east_store(i, j, load_b)
+            east_store(i, j, east_of(i, j), True)
         return carry
 
     def south_store(i, j, ref, start, gap):
         p = i * C + j
         o, w = do[i, j], dw[i, j]
-        base = PAD + p * 2 * S
+        base = rows_of(p)
+        _, third = weights(i, j, False)
 
         def piece(q):
-            keep = row8 >= o - q if q < S - 8 else row8 < o + w - q
-            b_re = ref[pl.ds(start + (q - o), 8), :]
-            b_im = ref[pl.ds(start + gap + (q - o), 8), :]
-            return (
-                pv[pl.ds(pl.multiple_of(base + q, 8), 8), :],
-                pv[pl.ds(pl.multiple_of(base + S + q, 8), 8), :],
-                jnp.where(keep, b_re, 0.0),
-                jnp.where(keep, b_im, 0.0),
-            )
+            keep = reached(i, j, q)
+            b_re = jnp.where(keep, ref[pl.ds(start + (q - o), 8), :], 0.0)
+            b_im = jnp.where(keep, ref[pl.ds(start + gap + (q - o), 8), :], 0.0)
+            to = p * 2 * T + q - lo
+            put_at(sw, to, b_re * third)
+            put_at(sw, to + T, b_im * third)
+            return at(pv, base + q), at(pv, base + S + q), b_re, b_im
 
         re, im = gathered(piece(q) for q in range(lo, S, 8))
         put(2, p, re, im, w)
 
     def south_inner(i, carry):
         for j in range(C):
-            south_store(i, j, pv, PAD + ((i + 1) * C + j) * 2 * S, S)
+            south_store(i, j, pv, rows_of((i + 1) * C + j), S)
         return carry
 
     spread(0)
@@ -246,7 +290,7 @@
         for k in range(2 * C):
             south_copy(k, my_row).wait_recv()
 
-    @pl.when(my_row == nr - 1)
+    @pl.when(last_row)
     def _():
         south_recv[...] = jnp.zeros_like(south_recv)
 
@@ -256,7 +300,7 @@
     for k in range(5, len(steps)):
         spread(k)
 
-    @pl.when(my_col == nc - 1)
+    @pl.when(last_col)
     def _():
         east_recv[...] = jnp.zeros_like(east_recv)
 
@@ -266,11 +310,7 @@
         def _():
             east_copy(i, my_col).wait_recv()
 
-        def load_b(q, o):
-            both = east_recv[pl.ds(i * S + q, 8), :]
-            return pltpu.roll(both, o, 1), pltpu.roll(both, lax.rem(o + H, S), 1)
-
-        east_store(i, C - 1, load_b)
+        east_store(i, C - 1, east_rim(i), False)
 
     sums = lax.dot_general(
         jnp.ones((8, S), f32), acc[...], (((1,), (1,)), ((), ())),
@@ -295,6 +335,23 @@
 
     for other in others:
         gather_copy(other, (my_row, my_col)).start()
+
+    def weigh(i, carry):
+        for j in range(C):
+            half, third = weights(i, j, False)
+            base, to = rows_of(i * C + j), (i * C + j) * 2 * S
+            for q in range(0, S, 8):
+                weight = weight_at(i, j, q, half, third)
+                put_at(aw, to + q, at(pv, base + q) * weight)
+                put_at(aw, to + S + q, at(pv, base + S + q) * weight)
+        half, third = weights(i, C - 1, True)
+        load, o = east_rim(i), ro[i, C - 1]
+        for q in range(0, S, 8):
+            place_east(i, C - 1, q, load(q, o), half, third)
+        return carry
+
+    lax.fori_loop(0, R, weigh, 0)
+
     for other in others:
         gather_copy(other, other).wait_recv()
 
@@ -333,7 +390,7 @@
     cs = (jnp.where(valid, south, 0.0), jnp.where(valid, roll(south, -R * C, 1), 0.0))
     cw = tuple(from_west(x) for x in ce)
     cn = tuple(from_north(x) for x in cs)
-    count = float(ndev * R * C)
+    mean = 1.0 / float(ndev * R * C)
 
     def times(a, b):
         return (a[0] * b[0] - a[1] * b[1], a[0] * b[1] + a[1] * b[0])
@@ -341,7 +398,9 @@
     def conj_times(a, b):
         return (a[0] * b[0] + a[1] * b[1], a[0] * b[1] - a[1] * b[0])
 
-    now = (jnp.ones((ndev, S), f32), jnp.zeros((ndev, S), f32))
+    now = (jnp.where(valid, f32(1.0), f32(0.0)), jnp.zeros((ndev, S), f32))
+    square = jnp.zeros((ndev, S), f32)
+    constant = 1.0
     for step in range(ITERS):
         terms = (
             times(ce, tuple(from_east(x) for x in now)),
@@ -349,20 +408,27 @@
             conj_times(cw, tuple(from_west(x) for x in now)),
             conj_times(cn, tuple(from_north(x) for x in now)),
         )
-        image = tuple(
+        now = tuple(
             jnp.where(valid, terms[0][q] + terms[1][q] + terms[2][q] + terms[3][q], 0.0)
             for q in range(2)
         )
-        total = jnp.sum(image[0] * image[0] + image[1] * image[1], axis=0, keepdims=True)
-        total = jnp.sum(total, axis=1, keepdims=True)
-        factor = 1.0 / jnp.sqrt(total / count + eps_norm)
-        now = (image[0] * factor, image[1] * factor)
+        square = eps_norm * square + (now[0] * now[0] + now[1] * now[1])
+        constant = constant * eps_norm
     outs = now + tuple(from_east(x) for x in now) + tuple(from_south(x) for x in now)
     for q in range(6):
         fields[q] = outs[q]
+    total = jnp.sum(jnp.sum(square, axis=0, keepdims=True), axis=1, keepdims=True)
+    factor = 1.0 / jnp.sqrt(total * mean + constant)
+    diagonal = lax.broadcasted_iota(jnp.int32, (R * C, S), 0) == lax.broadcasted_iota(
+        jnp.int32, (R * C, S), 1
+    )
     for q in range(6):
-        phase_out[q : q + 1, :] = fields[q, pl.ds(me, 1), :]
-    phase_out[6:8, :] = jnp.zeros((2, S), f32)
+        row = fields[q, pl.ds(me, 1), :] * factor
+        phase_out[q : q + 1, :] = row
+        spot = jnp.where(diagonal, jnp.broadcast_to(row, (R * C, S)), 0.0)
+        factors[q * R * C : (q + 1) * R * C, :] = jnp.broadcast_to(
+            jnp.sum(spot, axis=1, keepdims=True), (R * C, S)
+        )
 
     for other in others:
         gather_copy(other, (my_row, my_col)).wait_send()
@@ -378,122 +444,87 @@
             south_copy(k, my_row - 1).wait_send()
 
 
-def blend_kernel(
-    dims, pv, ev, sv, ro, rw, do, dw, g, out, phases, ov, out_sem,
-):
-    R, C, S, nr, nc = dims
-    H = S // 2
-    lo = H - 8
-    row_size = C * 2 * S
-    last_col = lax.axis_index("col") == nc - 1
-    last_row = lax.axis_index("row") == nr - 1
-
-    def save(i):
+def blend_kernel(dims, aw, ew, sw, factors, phase, out, phases, ov, pad, out_sem, phase_sem):
+    R, C, S, pair = dims
+    lo = S // 2 - 8
+    T = S - lo
+    piece = pair * 2 * S
+
+    def save(k):
         return pltpu.make_async_copy(
-            ov.at[pl.ds(i * row_size, row_size)],
-            out.at[pl.ds(i * row_size, row_size)],
-            out_sem.at[i],
-        )
-
-    lane = lax.broadcasted_iota(jnp.int32, (1, S), 1)
-    row8 = lax.broadcasted_iota(jnp.int32, (8, S), 0)
+            ov.at[pl.ds(k * piece, piece)], out.at[pl.ds(k * piece, piece)], out_sem.at[k]
+        )
 
     def at(ref, row):
         return ref[pl.ds(pl.multiple_of(row, 8), 8), :]
 
-    def place(i, j, east, ref, start, gap):
-        p = i * C + j
-        oe, we, os, ws = ro[i, j], rw[i, j], do[i, j], dw[i, j]
-        g_re, g_im = g[0, p], g[1, p]
-        ge_re, ge_im, gs_re, gs_im = g[2, p], g[3, p], g[4, p], g[5, p]
-        phases[0, i, j] = g_re
-        phases[1, i, j] = g_im
-        base = PAD + p * 2 * S
-        to = p * 2 * S
-        keep_e = (lane >= oe) & (lane < oe + we)
-        live_e = keep_e & jnp.logical_not((j == C - 1) & last_col)
-        half = jnp.where(live_e, f32(0.5), f32(1.0))
-        third = jnp.where(live_e, f32(1.0 / 3.0), f32(0.5))
-        down = jnp.logical_not((i == R - 1) & last_row)
-        third = jnp.where(jnp.full((1, S), down), third, half)
-        half, third = jnp.broadcast_to(half, (8, S)), jnp.broadcast_to(third, (8, S))
-        e_re = jnp.broadcast_to(jnp.where(keep_e, ge_re, 0.0), (8, S))
-        e_im = jnp.broadcast_to(jnp.where(keep_e, ge_im, 0.0), (8, S))
-        h_re, h_im, x_re, x_im = g_re * half, g_im * half, e_re * half, e_im * half
+    def times(g, a):
+        return g[0] * a[0] - g[1] * a[1], g[0] * a[1] + g[1] * a[0]
+
+    def place(p):
+        g, ge, gs = (
+            [jnp.broadcast_to(factors[pl.ds((2 * k + part) * R * C + p, 1), :], (8, S)) for part in range(2)]
+            for k in range(3)
+        )
+        base = p * 2 * S
         for q in range(0, S, 8):
-            a_re, a_im = at(pv, base + q), at(pv, base + S + q)
-            b_re, b_im = east(q, oe)
-            if q < lo:
-                n_re = (h_re * a_re - h_im * a_im) + (x_re * b_re - x_im * b_im)
-                n_im = (h_re * a_im + h_im * a_re) + (x_re * b_im + x_im * b_re)
-            else:
-                keep = row8 >= os - q if q < S - 8 else row8 < os + ws - q
-                s_re = ref[pl.ds(start + (q - os), 8), :]
-                s_im = ref[pl.ds(start + gap + (q - os), 8), :]
-                n_re = (g_re * a_re - g_im * a_im) + (e_re * b_re - e_im * b_im)
-                n_im = (g_re * a_im + g_im * a_re) + (e_re * b_im + e_im * b_re)
-                inv = jnp.where(keep, third, half)
-                n_re = (n_re + jnp.where(keep, gs_re * s_re - gs_im * s_im, 0.0)) * inv
-                n_im = (n_im + jnp.where(keep, gs_re * s_im + gs_im * s_re, 0.0)) * inv
-            ov[pl.ds(pl.multiple_of(to + q, 8), 8), :] = n_re
-            ov[pl.ds(pl.multiple_of(to + S + q, 8), 8), :] = n_im
-
-    def east_of(i, j):
-        base = PAD + (i * C + j + 1) * 2 * S
-
-        def east(q, o):
-            return pltpu.roll(at(pv, base + q), o, 1), pltpu.roll(at(pv, base + S + q), o, 1)
-
-        return east
-
-    def east_rim(i):
-        def east(q, o):
-            both = at(ev, i * S + q)
-            return pltpu.roll(both, o, 1), pltpu.roll(both, lax.rem(o + H, S), 1)
-
-        return east
-
-    def south_of(i, j):
-        return pv, PAD + ((i + 1) * C + j) * 2 * S, S
-
-    def south_rim(j):
-        return sv, PAD + j * 2 * H, H
-
-    def rows(i, carry):
-        for j in range(C):
-            place(i, j, east_of(i, j) if j < C - 1 else east_rim(i), *south_of(i, j))
-        save(i).start()
+            own = times(g, (at(aw, base + q), at(aw, base + S + q)))
+            east = times(ge, (at(ew, base + q), at(ew, base + S + q)))
+            sums = [own[part] + east[part] for part in range(2)]
+            if q >= lo:
+                down = p * 2 * T + q - lo
+                south = times(gs, (at(sw, down), at(sw, down + T)))
+                sums = [sums[part] + south[part] for part in range(2)]
+            ov[pl.ds(pl.multiple_of(base + q, 8), 8), :] = sums[0]
+            ov[pl.ds(pl.multiple_of(base + S + q, 8), 8), :] = sums[1]
+
+    def step(k, carry):
+        for n in range(pair):
+            place(k * pair + n)
+        save(k).start()
         return carry
 
-    lax.fori_loop(0, R - 1, rows, 0)
-    for j in range(C):
-        place(R - 1, j, east_of(R - 1, j) if j < C - 1 else east_rim(R - 1), *south_rim(j))
-    save(R - 1).start()
-    for i in range(R):
-        save(i).wait()
+    lax.fori_loop(0, R * C // pair, step, 0)
+
+    row8 = lax.broadcasted_iota(jnp.int32, (R, S), 0)
+    for part in range(2):
+        line = jnp.broadcast_to(phase[part : part + 1, :], (R, S))
+        plane = line
+        for i in range(1, R):
+            plane = jnp.where(row8 == i, pltpu.roll(line, S - i * C, 1), plane)
+        pad[part] = plane[:, :C]
+    send = pltpu.make_async_copy(pad, phases, phase_sem.at[0])
+    send.start()
+    for k in range(R * C // pair):
+        save(k).wait()
+    send.wait()
 
 
 def local(nr, nc, patches, right_offset, right_width, down_offset, down_width):
     R, C, _, S, _ = patches.shape
     H, ndev = S // 2, nr * nc
+    T = S - (H - 8)
     dims = (R, C, S, nr, nc)
     flat = patches.reshape(R * C * 2 * S, S)
     anyspec = pl.BlockSpec(memory_space=pl.ANY)
-    smem = pl.BlockSpec(memory_space=pltpu.SMEM)
     vmem = pl.BlockSpec(memory_space=pltpu.VMEM)
     dma = pltpu.SemaphoreType.DMA
     tables = (right_offset, right_width, down_offset, down_width)
-    pv, east_halo, south_halo, phase = pl.pallas_call(
+    parts = pl.pallas_call(
         functools.partial(sync_kernel, dims),
         out_shape=(
+            pltpu.VMEM((R * C * 2 * S, S), f32),
+            pltpu.VMEM((R * C * 2 * S, S), f32),
+            pltpu.VMEM((R * C * 2 * T, S), f32),
+            pltpu.VMEM((6 * R * C, S), f32),
+            pltpu.VMEM((8, S), f32),
+        ),
+        in_specs=[pl.BlockSpec(memory_space=pltpu.HBM)] * 5,
+        out_specs=(vmem,) * 5,
+        scratch_shapes=[
             pltpu.VMEM((PAD + R * C * 2 * S, S), f32),
             pltpu.VMEM((R * S, S), f32),
             pltpu.VMEM((2 * PAD + 2 * C * H, S), f32),
-            jax.ShapeDtypeStruct((8, S), f32),
-        ),
-        in_specs=[pl.BlockSpec(memory_space=pltpu.HBM)] * 5,
-        out_specs=(vmem,) * 4,
-        scratch_shapes=[
             pltpu.VMEM((R * S, S), f32),
             pltpu.VMEM((4 * R * C, S), f32),
             pltpu.VMEM((2, S), f32),
@@ -508,25 +539,28 @@
             pltpu.SemaphoreType.REGULAR((n_rounds(nr) + n_rounds(nc),)),
         ],
         compiler_params=pltpu.CompilerParams(
-            collective_id=0, has_side_effects=True, vmem_limit_bytes=16 << 20
+            collective_id=0, has_side_effects=True, vmem_limit_bytes=24 << 20
         ),
         name="sync_patches",
     )(*(pltpu.with_memory_space_constraint(x, pltpu.HBM) for x in (flat, *tables)))
+    pair = 2
     blended, phases = pl.pallas_call(
-        functools.partial(blend_kernel, dims),
+        functools.partial(blend_kernel, (R, C, S, pair)),
         out_shape=(
             jax.ShapeDtypeStruct((R * C * 2 * S, S), f32),
             jax.ShapeDtypeStruct((2, R, C), f32),
         ),
-        in_specs=[vmem] * 3 + [smem] * 5,
-        out_specs=(anyspec, smem),
+        in_specs=[vmem] * 5,
+        out_specs=(anyspec, anyspec),
         scratch_shapes=[
             pltpu.VMEM((R * C * 2 * S, S), f32),
-            dma((R,)),
+            pltpu.VMEM((2, R, C), f32),
+            dma((R * C // pair,)),
+            dma((1,)),
         ],
         compiler_params=pltpu.CompilerParams(vmem_limit_bytes=24 << 20),
         name="blend_patches",
-    )(pv, east_halo, south_halo, *tables, phase)
+    )(*parts)
     return blended.reshape(patches.shape), phases
 
 

time: 31.7 us -> 29 us (0.915)
  Pallas kernels: 30.8 us -> 28.2 us
    pallas_call x1, Pallas kernels: 6.23 us -> 3.73 us  [local(): pl.pallas_call(functools.partial(blend_kernel, (R, C, S, pair)), out_shap...]
where the time goes in v1:
time: 29 us; the launch traced here: 28.9 us
  Pallas kernels  28.2 us (97%)
  between operations  0.64 us (2%)
    pallas_call x1, Pallas kernels, local(): pl.pallas_call(functools.partial(sync_kernel, dims), out_shape=(pltpu.VME...  24.5 us
    pallas_call x1, Pallas kernels, local(): pl.pallas_call(functools.partial(blend_kernel, (R, C, S, pair)), out_shap...  3.73 us

profile of v1, /device:TPU:0, one launch (start us, length us, event | category | flops | bytes accessed | tf_op | source)
XLA Modules:
  0.0 28.9 jit_solution(14779493062031362381)
XLA Ops:
  0.6 24.5 %sync_patches.1 = (f32[16384,128]{1,0:T(8,128)S(1)}, f32[16384,128]{1,0:T(8,128)S(1)}, f32[9216,128]{1,0:T(8,128)S(1)}, f32[384,128]{1,0:T(8,128)S(1)}, f32[8,128]{1,0:T(8,128)S(1)}) custom-call(f32[16384,128]{1,0:T(8,128)} %bitcast.2, s32[8,8]{1,0:T(8,128)} %ro_in.1, s32[8,8]{1,0:T(8,128)} %rw_in.1, s32[8,8]{1,0:T(8,128)} %do_in.1, s32[8,8]{1,0:T(8,128)} %dw_in.1), custom_call_target="tpu_custom_call" | custom-call | tf_op jit(solution)/shard_map/sync_patches/pallas_call | solution.py:513
  25.1 3.7 %blend_patches.1 = (f32[16384,128]{1,0:T(8,128)}, f32[2,8,8]{2,1,0:T(8,128)}) custom-call(f32[16384,128]{1,0:T(8,128)S(1)} %get-tuple-element.9.aw, f32[16384,128]{1,0:T(8,128)S(1)} %get-tuple-element.10.ew, f32[9216,128]{1,0:T(8,128)S(1)} %get-tuple-element.11.sw, f32[384,128]{1,0:T(8,128)S(1)} %get-tuple-element.12.factors, ...), custom_call_target="tpu_custom_call" | custom-call | tf_op jit(solution)/shard_map/blend_patches/pallas_call | solution.py:547

commit v2 on v1

--- a/solution.py
+++ b/solution.py
@@ -33,6 +33,24 @@
     return rounds
 
 
+def groups(n, sizes):
+    runs, first = [], 0
+    while first < n:
+        size = sizes[min(len(runs), len(sizes) - 1)]
+        runs.append(range(first, min(n, first + size)))
+        first += size
+    return runs
+
+
+def load_groups(n):
+    return groups(n, (1, 1, 2, 4))
+
+
+def arrive_groups(n):
+    tail = min(n, 4)
+    return groups(n - tail, (4,)) + [range(n - tail + k, n - tail + k + 1) for k in range(tail)]
+
+
 def n_rounds(n):
     return len(doubling(0, n, lambda k: (0, 0)))
 
@@ -40,7 +58,7 @@
 def sync_kernel(
     dims, patches, ro_in, rw_in, do_in, dw_in, aw, ew, sw, factors, phase_out,
     pv, east_recv, south_recv,
-    epack, acc, send_buf, recv, fields, ro, rw, do, dw,
+    epack, acc, send_buf, recv, fields, table,
     col_sem, rest_sem, e_send, e_recv, s_send, s_recv, g_send, g_recv, table_sem, round_sem,
 ):
     R, C, S, nr, nc = dims
@@ -51,10 +69,14 @@
     me = my_row * nc + my_col
     last_col, last_row = my_col == nc - 1, my_row == nr - 1
 
+    low = my_col < nc // 2
     turn_rows = [lax.rem(my_row + k, nr) for k in range(nr)]
-    turn_cols = [lax.rem(my_col + k, nc) for k in range(nc)]
+    turn_cols = [lax.rem(my_col + jnp.where(low, nc - k, k), nc) for k in range(nc)]
     others = [
-        (turn_rows[a], turn_cols[b]) for a in range(nr) for b in range(nc) if a or b
+        (turn_rows[a], turn_cols[b])
+        for b in [*range(1, nc), 0]
+        for a in [*range(1, nr), 0]
+        if a or b
     ]
     barrier = pltpu.get_barrier_semaphore()
 
@@ -83,11 +105,12 @@
             if k + 1 < len(steps):
                 tell(k + 1)
 
+    load_sem = {i: g for g, run in enumerate(load_groups(R)) for i in run}
     cols = [
         pltpu.make_async_copy(
             patches.at[pl.ds(i * C * 2 * S, 2 * S)],
             pv.at[pl.ds(PAD + i * C * 2 * S, 2 * S)],
-            col_sem.at[i],
+            col_sem.at[load_sem[i]],
         )
         for i in range(R)
     ]
@@ -95,77 +118,102 @@
         pltpu.make_async_copy(
             patches.at[pl.ds((i * C + 1) * 2 * S, (C - 1) * 2 * S)],
             pv.at[pl.ds(PAD + (i * C + 1) * 2 * S, (C - 1) * 2 * S)],
-            rest_sem.at[i],
+            rest_sem.at[0],
         )
         for i in range(R)
     ]
     tables = [
-        pltpu.make_async_copy(here, there, table_sem.at[k])
-        for k, (here, there) in enumerate(zip((ro_in, rw_in, do_in, dw_in), (ro, rw, do, dw)))
+        pltpu.make_async_copy(here, table.at[k], table_sem.at[0])
+        for k, here in enumerate((ro_in, rw_in, do_in, dw_in))
     ]
+    ro, rw, do, dw = (table.at[k] for k in range(4))
+
+    def whole(src, dst, sem):
+        return pltpu.make_async_copy(src, dst, sem)
+
     for copy in cols:
         copy.start()
+    signal(barrier, my_row, my_col + 1, my_col < nc - 1)
     signal(barrier, my_row + 1, my_col, my_row < nr - 1)
-    signal(barrier, my_row, my_col + 1, my_col < nc - 1)
+    lane = lax.broadcasted_iota(jnp.int32, (S, S), 1)
+
+    def load(g):
+        size = len(load_groups(R)[g]) * 2 * S
+        whole(patches.at[pl.ds(0, size)], pv.at[pl.ds(PAD, size)], col_sem.at[g]).wait()
+
+    def pack(i):
+        base = PAD + i * C * 2 * S
+        re = pv[pl.ds(base, S), :]
+        im = pv[pl.ds(base + S, S), :]
+        epack[pl.ds(i * S, S), :] = jnp.where(lane < H, re, pltpu.roll(im, H, 1))
+
+    def south_copy(k, row):
+        return pltpu.make_async_remote_copy(
+            src_ref=patches.at[pl.ds(k * S, H)],
+            dst_ref=south_recv.at[pl.ds(PAD + k * H, H)],
+            send_sem=s_send.at[0],
+            recv_sem=s_recv.at[0],
+            device_id=(row, my_col),
+            device_id_type=MESH,
+        )
+
+    def all_south(row):
+        return pltpu.make_async_remote_copy(
+            src_ref=patches.at[pl.ds(0, 2 * C * H)],
+            dst_ref=south_recv.at[pl.ds(PAD, 2 * C * H)],
+            send_sem=s_send.at[0],
+            recv_sem=s_recv.at[0],
+            device_id=(row, my_col),
+            device_id_type=MESH,
+        )
+
+    arrive_sem = {i: g for g, run in enumerate(arrive_groups(R)) for i in run}
+
+    def east_run(first, n, sem, col):
+        return pltpu.make_async_remote_copy(
+            src_ref=epack.at[pl.ds(first * S, n * S)],
+            dst_ref=east_recv.at[pl.ds(first * S, n * S)],
+            send_sem=e_send.at[0],
+            recv_sem=e_recv.at[sem],
+            device_id=(my_row, col),
+            device_id_type=MESH,
+        )
+
+    def east_copy(k, col):
+        return east_run(k, 1, arrive_sem[k], col)
+
+    def send_east(i):
+        @pl.when(my_col > 0)
+        def _():
+            east_copy(i, my_col - 1).start()
+
+    load(0)
     for copy in tables:
         copy.start()
     for copy in rests:
         copy.start()
-    lane = lax.broadcasted_iota(jnp.int32, (S, S), 1)
-
-    def pack(i):
-        base = PAD + i * C * 2 * S
-        cols[i].wait()
-        re = pv[pl.ds(base, S), :]
-        im = pv[pl.ds(base + S, S), :]
-        epack[pl.ds(i * S, S), :] = jnp.where(lane < H, re, pltpu.roll(im, H, 1))
-
-    def south_copy(k, row):
-        return pltpu.make_async_remote_copy(
-            src_ref=patches.at[pl.ds(k * S, H)],
-            dst_ref=south_recv.at[pl.ds(PAD + k * H, H)],
-            send_sem=s_send.at[k],
-            recv_sem=s_recv.at[k],
-            device_id=(row, my_col),
-            device_id_type=MESH,
-        )
-
-    def east_copy(k, col):
-        return pltpu.make_async_remote_copy(
-            src_ref=epack.at[pl.ds(k * S, S)],
-            dst_ref=east_recv.at[pl.ds(k * S, S)],
-            send_sem=e_send.at[k],
-            recv_sem=e_recv.at[k],
-            device_id=(my_row, col),
-            device_id_type=MESH,
-        )
-
-    def send_east(i):
-        @pl.when(my_col > 0)
-        def _():
-            east_copy(i, my_col - 1).start()
-
-    for i in range(2):
-        pack(i)
+    pack(0)
     await_all(barrier, my_row > 0, my_col > 0)
-    for i in range(2):
-        send_east(i)
-
-    @pl.when(my_row > 0)
-    def _():
-        for k in range(2 * C):
-            south_copy(k, my_row - 1).start()
-
-    if steps:
-        tell(0)
-    for i in range(2, R):
-        pack(i)
-        send_east(i)
+    send_east(0)
+    for g, run in enumerate(load_groups(R)):
+        if g:
+            load(g)
+            for i in run:
+                pack(i)
+                send_east(i)
+        if g == 1 or len(load_groups(R)) == 1:
+
+            @pl.when(my_row > 0)
+            def _():
+                for k in range(2 * C):
+                    south_copy(k, my_row - 1).start()
+
+            if steps:
+                tell(0)
     acc[...] = jnp.zeros_like(acc)
-    for copy in tables:
-        copy.wait()
-    for copy in rests:
-        copy.wait()
+    whole(table, table, table_sem.at[0]).wait()
+    size = R * (C - 1) * 2 * S
+    whole(patches.at[pl.ds(0, size)], pv.at[pl.ds(PAD, size)], rest_sem.at[0]).wait()
 
     lane1 = lax.broadcasted_iota(jnp.int32, (1, S), 1)
     row8 = lax.broadcasted_iota(jnp.int32, (8, S), 0)
@@ -176,10 +224,14 @@
     def put_at(ref, row, value):
         ref[pl.ds(pl.multiple_of(row, 8), 8), :] = value
 
+    def scaled(re, im, width):
+        scale = 1.0 / jnp.sqrt(jnp.full((1, S), S * width, jnp.int32).astype(f32))
+        return fold_rows(re) * scale, fold_rows(im) * scale
+
     def put(plane, p, re, im, width):
-        scale = 1.0 / jnp.sqrt(jnp.full((1, S), S * width, jnp.int32).astype(f32))
-        acc[pl.ds(plane * R * C + p, 1), :] = fold_rows(re) * scale
-        acc[pl.ds((plane + 1) * R * C + p, 1), :] = fold_rows(im) * scale
+        re, im = scaled(re, im, width)
+        acc[pl.ds(plane * R * C + p, 1), :] = re
+        acc[pl.ds((plane + 1) * R * C + p, 1), :] = im
 
     def gathered(pieces):
         re, im = None, None
@@ -231,7 +283,7 @@
         put_at(ew, to, b[0] * weight)
         put_at(ew, to + S, b[1] * weight)
 
-    def east_store(i, j, load, place):
+    def east_sums(i, j, load, place):
         p = i * C + j
         o, w = ro[i, j], rw[i, j]
         base = rows_of(p)
@@ -245,11 +297,11 @@
 
         re, im = gathered(piece(q) for q in range(0, S, 8))
         keep = (lane1 >= o) & (lane1 < o + w)
-        put(0, p, jnp.where(keep, re, 0.0), jnp.where(keep, im, 0.0), w)
+        return p, jnp.where(keep, re, 0.0), jnp.where(keep, im, 0.0), w
 
     def east_inner(i, carry):
         for j in range(C - 1):
-            east_store(i, j, east_of(i, j), True)
+            put(0, *east_sums(i, j, east_of(i, j), True))
         return carry
 
     def south_store(i, j, ref, start, gap):
@@ -287,8 +339,7 @@
 
     @pl.when(my_row < nr - 1)
     def _():
-        for k in range(2 * C):
-            south_copy(k, my_row).wait_recv()
+        all_south(my_row).wait_recv()
 
     @pl.when(last_row)
     def _():
@@ -304,19 +355,30 @@
     def _():
         east_recv[...] = jnp.zeros_like(east_recv)
 
-    for i in range(R):
+    def east_arrive(g):
+        run = arrive_groups(R)[g]
 
         @pl.when(my_col < nc - 1)
         def _():
-            east_copy(i, my_col).wait_recv()
-
-        east_store(i, C - 1, east_rim(i), False)
+            east_run(run[0], len(run), g, my_col).wait_recv()
+
+        return run
+
+    last = len(arrive_groups(R)) - 1
+    for g in range(last):
+        for i in east_arrive(g):
+            put(0, *east_sums(i, C - 1, east_rim(i), False))
 
     sums = lax.dot_general(
         jnp.ones((8, S), f32), acc[...], (((1,), (1,)), ((), ())),
         precision=highest, preferred_element_type=f32,
     )
-    mine = jnp.concatenate([sums[0:1, :S], sums[0:1, S:]], axis=0)
+    east_row = sums[0:1, :S]
+    for i in east_arrive(last):
+        p, re, im, width = east_sums(i, C - 1, east_rim(i), False)
+        re, im = (jnp.sum(x, axis=1, keepdims=True) for x in scaled(re, im, width))
+        east_row = jnp.where(lane1 == p, re, jnp.where(lane1 == R * C + p, im, east_row))
+    mine = jnp.concatenate([east_row, sums[0:1, S:]], axis=0)
     send_buf[...] = mine
     recv[me] = mine
 
@@ -327,9 +389,19 @@
         return pltpu.make_async_remote_copy(
             src_ref=send_buf,
             dst_ref=recv.at[index(source)],
-            send_sem=g_send.at[index(target)],
-            recv_sem=g_recv.at[index(source)],
+            send_sem=g_send.at[0],
+            recv_sem=g_recv.at[0],
             device_id=target,
+            device_id_type=MESH,
+        )
+
+    def all_gathered():
+        return pltpu.make_async_remote_copy(
+            src_ref=recv.at[pl.ds(0, ndev - 1)],
+            dst_ref=recv.at[pl.ds(0, ndev - 1)],
+            send_sem=g_send.at[0],
+            recv_sem=g_recv.at[0],
+            device_id=others[0],
             device_id_type=MESH,
         )
 
@@ -352,8 +424,7 @@
 
     lax.fori_loop(0, R, weigh, 0)
 
-    for other in others:
-        gather_copy(other, other).wait_recv()
+    all_gathered().wait_recv()
 
     got = recv[...]
     east, south = got[:, 0, :], got[:, 1, :]
@@ -398,10 +469,11 @@
     def conj_times(a, b):
         return (a[0] * b[0] + a[1] * b[1], a[0] * b[1] - a[1] * b[0])
 
-    now = (jnp.where(valid, f32(1.0), f32(0.0)), jnp.zeros((ndev, S), f32))
-    square = jnp.zeros((ndev, S), f32)
-    constant = 1.0
-    for step in range(ITERS):
+    now = (ce[0] + cs[0] + cw[0] + cn[0], ce[1] + cs[1] - cw[1] - cn[1])
+    now = tuple(jnp.where(valid, x, 0.0) for x in now)
+    square = now[0] * now[0] + now[1] * now[1]
+    constant = eps_norm
+    for step in range(1, ITERS):
         terms = (
             times(ce, tuple(from_east(x) for x in now)),
             times(cs, tuple(from_south(x) for x in now)),
@@ -430,18 +502,15 @@
             jnp.sum(spot, axis=1, keepdims=True), (R * C, S)
         )
 
-    for other in others:
-        gather_copy(other, (my_row, my_col)).wait_send()
+    all_gathered().wait_send()
 
     @pl.when(my_col > 0)
     def _():
-        for k in range(R):
-            east_copy(k, my_col - 1).wait_send()
+        east_run(0, R, 0, my_col - 1).wait_send()
 
     @pl.when(my_row > 0)
     def _():
-        for k in range(2 * C):
-            south_copy(k, my_row - 1).wait_send()
+        all_south(my_row - 1).wait_send()
 
 
 def blend_kernel(dims, aw, ew, sw, factors, phase, out, phases, ov, pad, out_sem, phase_sem):
@@ -452,7 +521,7 @@
 
     def save(k):
         return pltpu.make_async_copy(
-            ov.at[pl.ds(k * piece, piece)], out.at[pl.ds(k * piece, piece)], out_sem.at[k]
+            ov.at[pl.ds(k * piece, piece)], out.at[pl.ds(k * piece, piece)], out_sem.at[0]
         )
 
     def at(ref, row):
@@ -495,9 +564,8 @@
         pad[part] = plane[:, :C]
     send = pltpu.make_async_copy(pad, phases, phase_sem.at[0])
     send.start()
-    for k in range(R * C // pair):
-        save(k).wait()
     send.wait()
+    pltpu.make_async_copy(ov, out, out_sem.at[0]).wait()
 
 
 def local(nr, nc, patches, right_offset, right_width, down_offset, down_width):
@@ -530,12 +598,12 @@
             pltpu.VMEM((2, S), f32),
             pltpu.VMEM((ndev, 2, S), f32),
             pltpu.VMEM((6, ndev, S), f32),
-        ] + [pltpu.SMEM((R, C), jnp.int32)] * 4 + [
-            dma((R,)), dma((R,)),
-            dma((R,)), dma((R,)),
-            dma((2 * C,)), dma((2 * C,)),
-            dma((ndev,)), dma((ndev,)),
-            dma((4,)),
+            pltpu.SMEM((4, R, C), jnp.int32),
+            dma((len(load_groups(R)),)), dma((1,)),
+            dma((1,)), dma((len(arrive_groups(R)),)),
+            dma((1,)), dma((1,)),
+            dma((1,)), dma((1,)),
+            dma((1,)),
             pltpu.SemaphoreType.REGULAR((n_rounds(nr) + n_rounds(nc),)),
         ],
         compiler_params=pltpu.CompilerParams(
@@ -555,7 +623,7 @@
         scratch_shapes=[
             pltpu.VMEM((R * C * 2 * S, S), f32),
             pltpu.VMEM((2, R, C), f32),
-            dma((R * C // pair,)),
+            dma((1,)),
             dma((1,)),
         ],
         compiler_params=pltpu.CompilerParams(vmem_limit_bytes=24 << 20),

time: 29 us -> 27.3 us (0.941)
  Pallas kernels: 28.2 us -> 26.5 us
    pallas_call x1, Pallas kernels: 24.5 us -> 23.1 us  [local(): pl.pallas_call(functools.partial(sync_kernel, dims), out_shape=(pltpu.VME...]
where the time goes in v2:
time: 27.3 us; the launch traced here: 27.2 us
  Pallas kernels  26.5 us (97%)
  between operations  0.64 us (2%)
    pallas_call x1, Pallas kernels, local(): pl.pallas_call(functools.partial(sync_kernel, dims), out_shape=(pltpu.VME...  23.1 us
    pallas_call x1, Pallas kernels, local(): pl.pallas_call(functools.partial(blend_kernel, (R, C, S, pair)), out_shap...  3.45 us

profile of v2, /device:TPU:0, one launch (start us, length us, event | category | flops | bytes accessed | tf_op | source)
XLA Modules:
  0.0 27.2 jit_solution(1867610285087019803)
XLA Ops:
  0.6 23.1 %sync_patches.1 = (f32[16384,128]{1,0:T(8,128)S(1)}, f32[16384,128]{1,0:T(8,128)S(1)}, f32[9216,128]{1,0:T(8,128)S(1)}, f32[384,128]{1,0:T(8,128)S(1)}, f32[8,128]{1,0:T(8,128)S(1)}) custom-call(f32[16384,128]{1,0:T(8,128)} %bitcast.2, s32[8,8]{1,0:T(8,128)} %ro_in.1, s32[8,8]{1,0:T(8,128)} %rw_in.1, s32[8,8]{1,0:T(8,128)} %do_in.1, s32[8,8]{1,0:T(8,128)} %dw_in.1), custom_call_target="tpu_custom_call" | custom-call | tf_op jit(solution)/shard_map/sync_patches/pallas_call | solution.py:581
  23.7 3.5 %blend_patches.1 = (f32[16384,128]{1,0:T(8,128)}, f32[2,8,8]{2,1,0:T(8,128)}) custom-call(f32[16384,128]{1,0:T(8,128)S(1)} %get-tuple-element.9.aw, f32[16384,128]{1,0:T(8,128)S(1)} %get-tuple-element.10.ew, f32[9216,128]{1,0:T(8,128)S(1)} %get-tuple-element.11.sw, f32[384,128]{1,0:T(8,128)S(1)} %get-tuple-element.12.factors, ...), custom_call_target="tpu_custom_call" | custom-call | tf_op jit(solution)/shard_map/blend_patches/pallas_call | solution.py:615

commit v3 on v2

--- a/solution.py
+++ b/solution.py
@@ -58,8 +58,9 @@
 def sync_kernel(
     dims, patches, ro_in, rw_in, do_in, dw_in, aw, ew, sw, factors, phase_out,
     pv, east_recv, south_recv,
-    epack, acc, send_buf, recv, fields, table,
+    epack, acc, send_buf, recv, fields, table, relay_buf, strips, turned, late,
     col_sem, rest_sem, e_send, e_recv, s_send, s_recv, g_send, g_recv, table_sem, round_sem,
+    relay_recv, relay_send, turn_recv, turn_send, pair_sem,
 ):
     R, C, S, nr, nc = dims
     H, ndev = S // 2, nr * nc
@@ -68,6 +69,22 @@
     my_row, my_col = lax.axis_index("row"), lax.axis_index("col")
     me = my_row * nc + my_col
     last_col, last_row = my_col == nc - 1, my_row == nr - 1
+    even = lax.rem(my_col, 2) == 0
+    opens = even & (my_col >= 2) & (my_col < nc - 1)
+    closes = jnp.logical_not(even) & (my_col >= 3)
+    n_relay, n_turn = R // 2, min(2, R)
+
+    def relayed(c):
+        return jnp.clip(c - 2, 0, n_relay)
+
+    def turned_of(c):
+        return jnp.where(c == nc - 2, n_turn, 1)
+
+    def sent_around(i):
+        return opens & (i >= R - relayed(my_col))
+
+    def turned_here(i):
+        return opens & (i >= R - turned_of(my_col))
 
     low = my_col < nc // 2
     turn_rows = [lax.rem(my_row + k, nr) for k in range(nr)]
@@ -183,9 +200,53 @@
         return east_run(k, 1, arrive_sem[k], col)
 
     def send_east(i):
-        @pl.when(my_col > 0)
+        @pl.when((my_col > 0) & jnp.logical_not(sent_around(i)) if i >= R - n_relay else my_col > 0)
         def _():
             east_copy(i, my_col - 1).start()
+
+    def relay_copy(i, col):
+        k = i - (R - n_relay)
+        return pltpu.make_async_remote_copy(
+            src_ref=epack.at[pl.ds(i * S, S)],
+            dst_ref=relay_buf.at[pl.ds(k * S, S)],
+            send_sem=e_send.at[0],
+            recv_sem=relay_recv.at[k],
+            device_id=(my_row, col),
+            device_id_type=MESH,
+        )
+
+    def forward_copy(i, col):
+        k = i - (R - n_relay)
+        return pltpu.make_async_remote_copy(
+            src_ref=relay_buf.at[pl.ds(k * S, S)],
+            dst_ref=east_recv.at[pl.ds(i * S, S)],
+            send_sem=relay_send.at[k],
+            recv_sem=e_recv.at[arrive_sem[i]],
+            device_id=(my_row, col),
+            device_id_type=MESH,
+        )
+
+    def forwards(i):
+        return closes & (i >= R - relayed(my_col - 1))
+
+    def forward(i):
+        if i < R:
+
+            @pl.when(forwards(i))
+            def _():
+                relay_copy(i, my_col).wait_recv()
+                forward_copy(i, my_col - 2).start()
+
+    def turn_copy(i, col):
+        k = i - (R - n_turn)
+        return pltpu.make_async_remote_copy(
+            src_ref=strips.at[pl.ds(k * S, S)],
+            dst_ref=turned.at[pl.ds(k * S, S)],
+            send_sem=turn_send.at[k],
+            recv_sem=turn_recv.at[k],
+            device_id=(my_row, col),
+            device_id_type=MESH,
+        )
 
     load(0)
     for copy in tables:
@@ -195,6 +256,7 @@
     pack(0)
     await_all(barrier, my_row > 0, my_col > 0)
     send_east(0)
+    signal(pair_sem.at[0], my_row, my_col - 1, closes)
     for g, run in enumerate(load_groups(R)):
         if g:
             load(g)
@@ -211,12 +273,34 @@
             if steps:
                 tell(0)
     acc[...] = jnp.zeros_like(acc)
+    late[...] = jnp.zeros_like(late)
+    await_all(pair_sem.at[0], opens)
+    for i in range(R - n_relay, R):
+
+        @pl.when(sent_around(i))
+        def _():
+            relay_copy(i, my_col + 1).start()
+
+    spread(0)
     whole(table, table, table_sem.at[0]).wait()
     size = R * (C - 1) * 2 * S
     whole(patches.at[pl.ds(0, size)], pv.at[pl.ds(PAD, size)], rest_sem.at[0]).wait()
 
     lane1 = lax.broadcasted_iota(jnp.int32, (1, S), 1)
     row8 = lax.broadcasted_iota(jnp.int32, (8, S), 0)
+
+    for i in range(R - n_turn, R):
+
+        @pl.when(turned_here(i))
+        def _():
+            o, w = ro[i, C - 1], rw[i, C - 1]
+            base = PAD + (i * C + C - 1) * 2 * S
+            scale = 1.0 / jnp.sqrt(jnp.full((1, S), S * w, jnp.int32).astype(f32))
+            weight = jnp.where((lane1 & (H - 1)) < w, scale, 0.0)
+            re = pltpu.roll(pv[pl.ds(base, S), :], S - o, 1)
+            im = pltpu.roll(pv[pl.ds(base + S, S), :], lax.rem(S + H - o, S), 1)
+            strips[pl.ds((i - R + n_turn) * S, S), :] = jnp.where(lane < H, re, im) * weight
+            turn_copy(i, my_col + 1).start()
 
     def at(ref, row):
         return ref[pl.ds(pl.multiple_of(row, 8), 8), :]
@@ -327,15 +411,20 @@
             south_store(i, j, pv, rows_of((i + 1) * C + j), S)
         return carry
 
-    spread(0)
+    spread(1)
     lax.fori_loop(0, R // 2, east_inner, 0)
-    spread(1)
+    spread(2)
+    forward(R - n_relay)
     lax.fori_loop(R // 2, R, east_inner, 0)
-    spread(2)
+    spread(3)
+    forward(R - n_relay + 1)
     lax.fori_loop(0, R // 2, south_inner, 0)
-    spread(3)
+    spread(4)
+    forward(R - n_relay + 2)
     lax.fori_loop(R // 2, R - 1, south_inner, 0)
-    spread(4)
+    spread(5)
+    for i in range(R - n_relay + 3, R):
+        forward(i)
 
     @pl.when(my_row < nr - 1)
     def _():
@@ -348,37 +437,78 @@
     for j in range(C):
         south_store(R - 1, j, south_recv, PAD + j * 2 * H, H)
 
-    for k in range(5, len(steps)):
+    for k in range(6, len(steps)):
         spread(k)
 
     @pl.when(last_col)
     def _():
         east_recv[...] = jnp.zeros_like(east_recv)
 
-    def east_arrive(g):
+    def east_wait(g):
         run = arrive_groups(R)[g]
-
-        @pl.when(my_col < nc - 1)
-        def _():
-            east_run(run[0], len(run), g, my_col).wait_recv()
-
-        return run
-
-    last = len(arrive_groups(R)) - 1
-    for g in range(last):
-        for i in east_arrive(g):
-            put(0, *east_sums(i, C - 1, east_rim(i), False))
-
+        east_run(run[0], len(run), g, my_col).wait_recv()
+
+    def rim_row(i):
+        return 2 * (i - (R - n_late))
+
+    n_late = min(3, R)
+    for g, run in enumerate(arrive_groups(R)):
+        if len(run) > 1 or run[0] < R - n_late:
+
+            @pl.when(jnp.logical_not(last_col))
+            def _():
+                east_wait(g)
+
+            for i in run:
+                put(0, *east_sums(i, C - 1, east_rim(i), False))
     sums = lax.dot_general(
         jnp.ones((8, S), f32), acc[...], (((1,), (1,)), ((), ())),
         precision=highest, preferred_element_type=f32,
     )
-    east_row = sums[0:1, :S]
-    for i in east_arrive(last):
-        p, re, im, width = east_sums(i, C - 1, east_rim(i), False)
-        re, im = (jnp.sum(x, axis=1, keepdims=True) for x in scaled(re, im, width))
-        east_row = jnp.where(lane1 == p, re, jnp.where(lane1 == R * C + p, im, east_row))
-    mine = jnp.concatenate([east_row, sums[0:1, S:]], axis=0)
+
+    def rim(i):
+        @pl.when(jnp.logical_not(last_col) & jnp.logical_not(turned_here(i)))
+        def _():
+            east_wait(arrive_sem[i])
+            _, re, im, width = east_sums(i, C - 1, east_rim(i), False)
+            re, im = scaled(re, im, width)
+            late[rim_row(i) : rim_row(i) + 1, :] = re
+            late[rim_row(i) + 1 : rim_row(i) + 2, :] = im
+
+    def turn_row(i):
+        return 2 * n_late + 2 * (i - (R - n_turn))
+
+    def turn(i):
+        @pl.when(closes & (i >= R - turned_of(my_col - 1)))
+        def _():
+            turn_copy(i, my_col).wait_recv()
+            re, im = None, None
+            for q in range(0, S, 8):
+                a = at(turned, (i - R + n_turn) * S + q)
+                b = at(epack, i * S + q)
+                u, v = a * b, a * pltpu.roll(b, H, 1)
+                re, im = (u, v) if re is None else (re + u, im + v)
+            im = jnp.where(lane1 < H, im, -im)
+            late[turn_row(i) : turn_row(i) + 1, :] = fold_rows(re)
+            late[turn_row(i) + 1 : turn_row(i) + 2, :] = fold_rows(im)
+
+    for i in range(R - n_late, R):
+        if i == R - 1:
+            for k in range(R - n_turn, R):
+                turn(k)
+        rim(i)
+    tails = jnp.sum(late[...], axis=1, keepdims=True)
+
+    def spot(i, part, row):
+        return jnp.where(lane1 == part * R * C + i * C + C - 1, tails[row : row + 1, :], 0.0)
+
+    east_row, turn_line = sums[0:1, :S], jnp.zeros((1, S), f32)
+    for part in range(2):
+        for i in range(R - n_late, R):
+            east_row = east_row + spot(i, part, rim_row(i) + part)
+        for i in range(R - n_turn, R):
+            turn_line = turn_line + spot(i, part, turn_row(i) + part)
+    mine = jnp.concatenate([east_row, sums[0:1, S:], turn_line], axis=0)
     send_buf[...] = mine
     recv[me] = mine
 
@@ -416,6 +546,9 @@
                 weight = weight_at(i, j, q, half, third)
                 put_at(aw, to + q, at(pv, base + q) * weight)
                 put_at(aw, to + S + q, at(pv, base + S + q) * weight)
+        return carry
+
+    def weigh_rim(i, carry):
         half, third = weights(i, C - 1, True)
         load, o = east_rim(i), ro[i, C - 1]
         for q in range(0, S, 8):
@@ -423,11 +556,18 @@
         return carry
 
     lax.fori_loop(0, R, weigh, 0)
+    for i in range(R - n_turn, R):
+
+        @pl.when(turned_here(i))
+        def _():
+            east_wait(arrive_sem[i])
+
+    lax.fori_loop(0, R, weigh_rim, 0)
 
     all_gathered().wait_recv()
 
     got = recv[...]
-    east, south = got[:, 0, :], got[:, 1, :]
+    east, south = got[:, 0, :] + pltpu.roll(got[:, 2, :], ndev - 1, 0), got[:, 1, :]
     field = lax.broadcasted_iota(jnp.int32, (ndev, S), 0)
     slot = lax.broadcasted_iota(jnp.int32, (ndev, S), 1)
     valid = slot < R * C
@@ -507,6 +647,18 @@
     @pl.when(my_col > 0)
     def _():
         east_run(0, R, 0, my_col - 1).wait_send()
+
+    for i in range(R - n_relay, R):
+
+        @pl.when(forwards(i))
+        def _():
+            forward_copy(i, my_col - 2).wait_send()
+
+    for i in range(R - n_turn, R):
+
+        @pl.when(turned_here(i))
+        def _():
+            turn_copy(i, my_col + 1).wait_send()
 
     @pl.when(my_row > 0)
     def _():
@@ -595,16 +747,23 @@
             pltpu.VMEM((2 * PAD + 2 * C * H, S), f32),
             pltpu.VMEM((R * S, S), f32),
             pltpu.VMEM((4 * R * C, S), f32),
-            pltpu.VMEM((2, S), f32),
-            pltpu.VMEM((ndev, 2, S), f32),
+            pltpu.VMEM((3, S), f32),
+            pltpu.VMEM((ndev, 3, S), f32),
             pltpu.VMEM((6, ndev, S), f32),
             pltpu.SMEM((4, R, C), jnp.int32),
+            pltpu.VMEM((R // 2 * S, S), f32),
+            pltpu.VMEM((min(2, R) * S, S), f32),
+            pltpu.VMEM((min(2, R) * S, S), f32),
+            pltpu.VMEM((16, S), f32),
             dma((len(load_groups(R)),)), dma((1,)),
             dma((1,)), dma((len(arrive_groups(R)),)),
             dma((1,)), dma((1,)),
             dma((1,)), dma((1,)),
             dma((1,)),
             pltpu.SemaphoreType.REGULAR((n_rounds(nr) + n_rounds(nc),)),
+            dma((R // 2,)), dma((R // 2,)),
+            dma((min(2, R),)), dma((min(2, R),)),
+            pltpu.SemaphoreType.REGULAR((1,)),
         ],
         compiler_params=pltpu.CompilerParams(
             collective_id=0, has_side_effects=True, vmem_limit_bytes=24 << 20

time: 27.3 us -> 27.9 us (1.022)
  Pallas kernels: 26.5 us -> 27.1 us
    pallas_call x1, Pallas kernels: 23.1 us -> 23.6 us  [local(): pl.pallas_call(functools.partial(sync_kernel, dims), out_shape=(pltpu.VME...]
where the time goes in v3:
time: 27.9 us; the launch traced here: 27.7 us
  Pallas kernels  27.1 us (97%)
  between operations  0.64 us (2%)
    pallas_call x1, Pallas kernels, local(): pl.pallas_call(functools.partial(sync_kernel, dims), out_shape=(pltpu.VME...  23.6 us
    pallas_call x1, Pallas kernels, local(): pl.pallas_call(functools.partial(blend_kernel, (R, C, S, pair)), out_shap...  3.45 us

profile of v3, /device:TPU:0, one launch (start us, length us, event | category | flops | bytes accessed | tf_op | source)
XLA Modules:
  0.0 27.7 jit_solution(14761577587135413169)
XLA Ops:
  0.6 23.6 %sync_patches.1 = (f32[16384,128]{1,0:T(8,128)S(1)}, f32[16384,128]{1,0:T(8,128)S(1)}, f32[9216,128]{1,0:T(8,128)S(1)}, f32[384,128]{1,0:T(8,128)S(1)}, f32[8,128]{1,0:T(8,128)S(1)}) custom-call(f32[16384,128]{1,0:T(8,128)} %bitcast.2, s32[8,8]{1,0:T(8,128)} %ro_in.1, s32[8,8]{1,0:T(8,128)} %rw_in.1, s32[8,8]{1,0:T(8,128)} %do_in.1, s32[8,8]{1,0:T(8,128)} %dw_in.1), custom_call_target="tpu_custom_call" | custom-call | tf_op jit(solution)/shard_map/sync_patches/pallas_call | solution.py:733
  24.3 3.5 %blend_patches.1 = (f32[16384,128]{1,0:T(8,128)}, f32[2,8,8]{2,1,0:T(8,128)}) custom-call(f32[16384,128]{1,0:T(8,128)S(1)} %get-tuple-element.9.aw, f32[16384,128]{1,0:T(8,128)S(1)} %get-tuple-element.10.ew, f32[9216,128]{1,0:T(8,128)S(1)} %get-tuple-element.11.sw, f32[384,128]{1,0:T(8,128)S(1)} %get-tuple-element.12.factors, ...), custom_call_target="tpu_custom_call" | custom-call | tf_op jit(solution)/shard_map/blend_patches/pallas_call | solution.py:774

commit v4 on v3

--- a/solution.py
+++ b/solution.py
@@ -40,6 +40,10 @@
         runs.append(range(first, min(n, first + size)))
         first += size
     return runs
+
+
+def n_relays(n):
+    return min(3, n // 2)
 
 
 def load_groups(n):
@@ -70,12 +74,12 @@
     me = my_row * nc + my_col
     last_col, last_row = my_col == nc - 1, my_row == nr - 1
     even = lax.rem(my_col, 2) == 0
-    opens = even & (my_col >= 2) & (my_col < nc - 1)
-    closes = jnp.logical_not(even) & (my_col >= 3)
-    n_relay, n_turn = R // 2, min(2, R)
+    opens = even & (my_col >= max(2, nc - 4)) & (my_col < nc - 1)
+    closes = jnp.logical_not(even) & (my_col >= max(3, nc - 3))
+    n_relay, n_turn = n_relays(R), min(2, R)
 
     def relayed(c):
-        return jnp.clip(c - 2, 0, n_relay)
+        return jnp.where(c == nc - 2, n_relay, 0)
 
     def turned_of(c):
         return jnp.where(c == nc - 2, n_turn, 1)
@@ -248,15 +252,23 @@
             device_id_type=MESH,
         )
 
+    @pl.when(closes)
+    def _():
+        await_all(barrier, my_row > 0, my_col > 0)
+        signal(pair_sem.at[0], my_row, my_col - 1, closes)
+
     load(0)
     for copy in tables:
         copy.start()
     for copy in rests:
         copy.start()
     pack(0)
-    await_all(barrier, my_row > 0, my_col > 0)
+
+    @pl.when(jnp.logical_not(closes))
+    def _():
+        await_all(barrier, my_row > 0, my_col > 0)
+
     send_east(0)
-    signal(pair_sem.at[0], my_row, my_col - 1, closes)
     for g, run in enumerate(load_groups(R)):
         if g:
             load(g)
@@ -423,8 +435,6 @@
     forward(R - n_relay + 2)
     lax.fori_loop(R // 2, R - 1, south_inner, 0)
     spread(5)
-    for i in range(R - n_relay + 3, R):
-        forward(i)
 
     @pl.when(my_row < nr - 1)
     def _():
@@ -751,7 +761,7 @@
             pltpu.VMEM((ndev, 3, S), f32),
             pltpu.VMEM((6, ndev, S), f32),
             pltpu.SMEM((4, R, C), jnp.int32),
-            pltpu.VMEM((R // 2 * S, S), f32),
+            pltpu.VMEM((n_relays(R) * S, S), f32),
             pltpu.VMEM((min(2, R) * S, S), f32),
             pltpu.VMEM((min(2, R) * S, S), f32),
             pltpu.VMEM((16, S), f32),
@@ -761,7 +771,7 @@
             dma((1,)), dma((1,)),
             dma((1,)),
             pltpu.SemaphoreType.REGULAR((n_rounds(nr) + n_rounds(nc),)),
-            dma((R // 2,)), dma((R // 2,)),
+            dma((n_relays(R),)), dma((n_relays(R),)),
             dma((min(2, R),)), dma((min(2, R),)),
             pltpu.SemaphoreType.REGULAR((1,)),
         ],

time: 27.9 us -> 26.7 us (0.957)
  Pallas kernels: 27.1 us -> 26 us
    pallas_call x1, Pallas kernels: 23.6 us -> 22.5 us  [local(): pl.pallas_call(functools.partial(sync_kernel, dims), out_shape=(pltpu.VME...]
where the time goes in v4:
time: 26.7 us; the launch traced here: 26.6 us
  Pallas kernels  26 us (97%)
  between operations  0.64 us (2%)
    pallas_call x1, Pallas kernels, local(): pl.pallas_call(functools.partial(sync_kernel, dims), out_shape=(pltpu.VME...  22.5 us
    pallas_call x1, Pallas kernels, local(): pl.pallas_call(functools.partial(blend_kernel, (R, C, S, pair)), out_shap...  3.45 us

profile of v4, /device:TPU:0, one launch (start us, length us, event | category | flops | bytes accessed | tf_op | source)
XLA Modules:
  0.0 26.6 jit_solution(7575964369667869428)
XLA Ops:
  0.6 22.5 %sync_patches.1 = (f32[16384,128]{1,0:T(8,128)S(1)}, f32[16384,128]{1,0:T(8,128)S(1)}, f32[9216,128]{1,0:T(8,128)S(1)}, f32[384,128]{1,0:T(8,128)S(1)}, f32[8,128]{1,0:T(8,128)S(1)}) custom-call(f32[16384,128]{1,0:T(8,128)} %bitcast.2, s32[8,8]{1,0:T(8,128)} %ro_in.1, s32[8,8]{1,0:T(8,128)} %rw_in.1, s32[8,8]{1,0:T(8,128)} %do_in.1, s32[8,8]{1,0:T(8,128)} %dw_in.1), custom_call_target="tpu_custom_call" | custom-call | tf_op jit(solution)/shard_map/sync_patches/pallas_call | solution.py:743
  23.1 3.5 %blend_patches.1 = (f32[16384,128]{1,0:T(8,128)}, f32[2,8,8]{2,1,0:T(8,128)}) custom-call(f32[16384,128]{1,0:T(8,128)S(1)} %get-tuple-element.9.aw, f32[16384,128]{1,0:T(8,128)S(1)} %get-tuple-element.10.ew, f32[9216,128]{1,0:T(8,128)S(1)} %get-tuple-element.11.sw, f32[384,128]{1,0:T(8,128)S(1)} %get-tuple-element.12.factors, ...), custom_call_target="tpu_custom_call" | custom-call | tf_op jit(solution)/shard_map/blend_patches/pallas_call | solution.py:784

commit v5 on v4

--- a/solution.py
+++ b/solution.py
@@ -51,8 +51,14 @@
 
 
 def arrive_groups(n):
-    tail = min(n, 4)
-    return groups(n - tail, (4,)) + [range(n - tail + k, n - tail + k + 1) for k in range(tail)]
+    return groups(n - 2, (max(1, n - 4), 2)) + [range(n - 2, n - 1), range(n - 1, n)] if n > 4 else groups(n, (1,))
+
+
+def send_runs(n):
+    runs = []
+    for run in arrive_groups(n):
+        runs += [run[:1], run[1:]] if run[0] == 0 and len(run) > 1 else [run]
+    return runs
 
 
 def n_rounds(n):
@@ -90,15 +96,11 @@
     def turned_here(i):
         return opens & (i >= R - turned_of(my_col))
 
-    low = my_col < nc // 2
-    turn_rows = [lax.rem(my_row + k, nr) for k in range(nr)]
-    turn_cols = [lax.rem(my_col + jnp.where(low, nc - k, k), nc) for k in range(nc)]
-    others = [
-        (turn_rows[a], turn_cols[b])
-        for b in [*range(1, nc), 0]
-        for a in [*range(1, nr), 0]
-        if a or b
-    ]
+    def skip(k, mine):
+        return k + (k >= mine).astype(jnp.int32)
+
+    others = [(a, skip(b, my_col)) for b in range(nc - 1) for a in range(nr)]
+    others += [(skip(a, my_row), my_col) for a in range(nr - 1)]
     barrier = pltpu.get_barrier_semaphore()
 
     def signal(sem, row, col, there):
@@ -152,9 +154,9 @@
     def whole(src, dst, sem):
         return pltpu.make_async_copy(src, dst, sem)
 
+    signal(barrier, my_row, my_col + 1, my_col < nc - 1)
     for copy in cols:
         copy.start()
-    signal(barrier, my_row, my_col + 1, my_col < nc - 1)
     signal(barrier, my_row + 1, my_col, my_row < nr - 1)
     lane = lax.broadcasted_iota(jnp.int32, (S, S), 1)
 
@@ -203,10 +205,19 @@
     def east_copy(k, col):
         return east_run(k, 1, arrive_sem[k], col)
 
-    def send_east(i):
-        @pl.when((my_col > 0) & jnp.logical_not(sent_around(i)) if i >= R - n_relay else my_col > 0)
-        def _():
-            east_copy(i, my_col - 1).start()
+    def send_east(run):
+        around = sent_around(run[-1]) if run[-1] >= R - n_relay else False
+
+        @pl.when((my_col > 0) & jnp.logical_not(around))
+        def _():
+            east_run(run[0], len(run), arrive_sem[run[0]], my_col - 1).start()
+
+        if len(run) > 1 and run[-1] >= R - n_relay:
+            for i in run:
+
+                @pl.when(around & jnp.logical_not(sent_around(i)))
+                def _():
+                    east_copy(i, my_col - 1).start()
 
     def relay_copy(i, col):
         k = i - (R - n_relay)
@@ -268,13 +279,16 @@
     def _():
         await_all(barrier, my_row > 0, my_col > 0)
 
-    send_east(0)
+    send_east(send_runs(R)[0])
+    sent = 1
     for g, run in enumerate(load_groups(R)):
         if g:
             load(g)
             for i in run:
                 pack(i)
-                send_east(i)
+                if i == send_runs(R)[sent][-1]:
+                    send_east(send_runs(R)[sent])
+                    sent += 1
         if g == 1 or len(load_groups(R)) == 1:
 
             @pl.when(my_row > 0)
@@ -461,9 +475,9 @@
     def rim_row(i):
         return 2 * (i - (R - n_late))
 
-    n_late = min(3, R)
+    n_late = min(2, R)
     for g, run in enumerate(arrive_groups(R)):
-        if len(run) > 1 or run[0] < R - n_late:
+        if run[-1] < R - n_late:
 
             @pl.when(jnp.logical_not(last_col))
             def _():
@@ -645,11 +659,11 @@
         jnp.int32, (R * C, S), 1
     )
     for q in range(6):
-        row = fields[q, pl.ds(me, 1), :] * factor
-        phase_out[q : q + 1, :] = row
-        spot = jnp.where(diagonal, jnp.broadcast_to(row, (R * C, S)), 0.0)
-        factors[q * R * C : (q + 1) * R * C, :] = jnp.broadcast_to(
-            jnp.sum(spot, axis=1, keepdims=True), (R * C, S)
+        row = fields[q, pl.ds(me, 1), :]
+        phase_out[q : q + 1, :] = row * factor
+        only = jnp.where(diagonal, jnp.broadcast_to(row, (R * C, S)), 0.0)
+        factors[q * R * C : (q + 1) * R * C, :] = (
+            jnp.broadcast_to(jnp.sum(only, axis=1, keepdims=True), (R * C, S)) * factor
         )
 
     all_gathered().wait_send()

time: 26.7 us -> 26.3 us (0.985)
  Pallas kernels: 26 us -> 25.6 us
    pallas_call x1, Pallas kernels: 22.5 us -> 22.1 us  [local(): pl.pallas_call(functools.partial(sync_kernel, dims), out_shape=(pltpu.VME...]
where the time goes in v5:
time: 26.3 us; the launch traced here: 26.2 us
  Pallas kernels  25.6 us (97%)
  between operations  0.64 us (2%)
    pallas_call x1, Pallas kernels, local(): pl.pallas_call(functools.partial(sync_kernel, dims), out_shape=(pltpu.VME...  22.1 us
    pallas_call x1, Pallas kernels, local(): pl.pallas_call(functools.partial(blend_kernel, (R, C, S, pair)), out_shap...  3.45 us

profile of v5, /device:TPU:0, one launch (start us, length us, event | category | flops | bytes accessed | tf_op | source)
XLA Modules:
  0.0 26.2 jit_solution(8785997109123850165)
XLA Ops:
  0.6 22.1 %sync_patches.1 = (f32[16384,128]{1,0:T(8,128)S(1)}, f32[16384,128]{1,0:T(8,128)S(1)}, f32[9216,128]{1,0:T(8,128)S(1)}, f32[384,128]{1,0:T(8,128)S(1)}, f32[8,128]{1,0:T(8,128)S(1)}) custom-call(f32[16384,128]{1,0:T(8,128)} %bitcast.2, s32[8,8]{1,0:T(8,128)} %ro_in.1, s32[8,8]{1,0:T(8,128)} %rw_in.1, s32[8,8]{1,0:T(8,128)} %do_in.1, s32[8,8]{1,0:T(8,128)} %dw_in.1), custom_call_target="tpu_custom_call" | custom-call | tf_op jit(solution)/shard_map/sync_patches/pallas_call | solution.py:757
  22.7 3.5 %blend_patches.1 = (f32[16384,128]{1,0:T(8,128)}, f32[2,8,8]{2,1,0:T(8,128)}) custom-call(f32[16384,128]{1,0:T(8,128)S(1)} %get-tuple-element.9.aw, f32[16384,128]{1,0:T(8,128)S(1)} %get-tuple-element.10.ew, f32[9216,128]{1,0:T(8,128)S(1)} %get-tuple-element.11.sw, f32[384,128]{1,0:T(8,128)S(1)} %get-tuple-element.12.factors, ...), custom_call_target="tpu_custom_call" | custom-call | tf_op jit(solution)/shard_map/blend_patches/pallas_call | solution.py:798

commit v6 on v5

--- a/solution.py
+++ b/solution.py
@@ -70,7 +70,7 @@
     pv, east_recv, south_recv,
     epack, acc, send_buf, recv, fields, table, relay_buf, strips, turned, late,
     col_sem, rest_sem, e_send, e_recv, s_send, s_recv, g_send, g_recv, table_sem, round_sem,
-    relay_recv, relay_send, turn_recv, turn_send, pair_sem,
+    relay_recv, turn_recv, pair_sem,
 ):
     R, C, S, nr, nc = dims
     H, ndev = S // 2, nr * nc
@@ -235,7 +235,7 @@
         return pltpu.make_async_remote_copy(
             src_ref=relay_buf.at[pl.ds(k * S, S)],
             dst_ref=east_recv.at[pl.ds(i * S, S)],
-            send_sem=relay_send.at[k],
+            send_sem=e_send.at[0],
             recv_sem=e_recv.at[arrive_sem[i]],
             device_id=(my_row, col),
             device_id_type=MESH,
@@ -257,7 +257,7 @@
         return pltpu.make_async_remote_copy(
             src_ref=strips.at[pl.ds(k * S, S)],
             dst_ref=turned.at[pl.ds(k * S, S)],
-            send_sem=turn_send.at[k],
+            send_sem=e_send.at[0],
             recv_sem=turn_recv.at[k],
             device_id=(my_row, col),
             device_id_type=MESH,
@@ -532,9 +532,9 @@
             east_row = east_row + spot(i, part, rim_row(i) + part)
         for i in range(R - n_turn, R):
             turn_line = turn_line + spot(i, part, turn_row(i) + part)
-    mine = jnp.concatenate([east_row, sums[0:1, S:], turn_line], axis=0)
-    send_buf[...] = mine
-    recv[me] = mine
+    for k, row in enumerate((east_row, sums[0:1, S:], turn_line)):
+        send_buf[k] = row
+        recv[k, pl.ds(me, 1), :] = row
 
     def index(d):
         return d[0] * nc + d[1]
@@ -542,7 +542,7 @@
     def gather_copy(target, source):
         return pltpu.make_async_remote_copy(
             src_ref=send_buf,
-            dst_ref=recv.at[index(source)],
+            dst_ref=recv.at[:, pl.ds(index(source), 1), :],
             send_sem=g_send.at[0],
             recv_sem=g_recv.at[0],
             device_id=target,
@@ -551,8 +551,8 @@
 
     def all_gathered():
         return pltpu.make_async_remote_copy(
-            src_ref=recv.at[pl.ds(0, ndev - 1)],
-            dst_ref=recv.at[pl.ds(0, ndev - 1)],
+            src_ref=recv.at[:, pl.ds(0, ndev - 1), :],
+            dst_ref=recv.at[:, pl.ds(0, ndev - 1), :],
             send_sem=g_send.at[0],
             recv_sem=g_recv.at[0],
             device_id=others[0],
@@ -590,11 +590,10 @@
 
     all_gathered().wait_recv()
 
-    got = recv[...]
-    east, south = got[:, 0, :] + pltpu.roll(got[:, 2, :], ndev - 1, 0), got[:, 1, :]
+    east, south = recv[0] + pltpu.roll(recv[2], ndev - 1, 0), recv[1]
     field = lax.broadcasted_iota(jnp.int32, (ndev, S), 0)
     slot = lax.broadcasted_iota(jnp.int32, (ndev, S), 1)
-    valid = slot < R * C
+    real = slot < R * C
     j_of, i_of = slot % C, (slot // C) % R
     dc, dr = field % nc, field // nc
 
@@ -621,68 +620,85 @@
         far = jnp.where(dr > 0, far, 0.0)
         return jnp.where(i_of > 0, roll(x, C, 1), far)
 
-    ce = (jnp.where(valid, east, 0.0), jnp.where(valid, roll(east, -R * C, 1), 0.0))
-    cs = (jnp.where(valid, south, 0.0), jnp.where(valid, roll(south, -R * C, 1), 0.0))
-    cw = tuple(from_west(x) for x in ce)
-    cn = tuple(from_north(x) for x in cs)
-    mean = 1.0 / float(ndev * R * C)
-
-    def times(a, b):
-        return (a[0] * b[0] - a[1] * b[1], a[0] * b[1] + a[1] * b[0])
-
-    def conj_times(a, b):
-        return (a[0] * b[0] + a[1] * b[1], a[0] * b[1] - a[1] * b[0])
-
-    now = (ce[0] + cs[0] + cw[0] + cn[0], ce[1] + cs[1] - cw[1] - cn[1])
-    now = tuple(jnp.where(valid, x, 0.0) for x in now)
-    square = now[0] * now[0] + now[1] * now[1]
+    def swap(x):
+        return roll(x, R * C, 1)
+
+    def conj(x):
+        return jnp.where(real, x, -x)
+
+    steps_to = (
+        (east, from_east),
+        (south, from_south),
+        (conj(from_west(east)), from_west),
+        (conj(from_north(south)), from_north),
+    )
+    straight, crossed = [], []
+    for corr, _ in steps_to:
+        other = swap(corr)
+        straight.append(jnp.where(real, corr, other))
+        crossed.append(jnp.where(real, other, -corr))
+
+    now = sum(corr for corr, _ in steps_to)
+    square = now * now
     constant = eps_norm
     for step in range(1, ITERS):
-        terms = (
-            times(ce, tuple(from_east(x) for x in now)),
-            times(cs, tuple(from_south(x) for x in now)),
-            conj_times(cw, tuple(from_west(x) for x in now)),
-            conj_times(cn, tuple(from_north(x) for x in now)),
-        )
-        now = tuple(
-            jnp.where(valid, terms[0][q] + terms[1][q] + terms[2][q] + terms[3][q], 0.0)
-            for q in range(2)
-        )
-        square = eps_norm * square + (now[0] * now[0] + now[1] * now[1])
+        moved = [move(now) for _, move in steps_to]
+        now = sum(a * b for a, b in zip(straight, moved))
+        now = now + swap(sum(a * b for a, b in zip(crossed, moved)))
+        square = eps_norm * square + now * now
         constant = constant * eps_norm
-    outs = now + tuple(from_east(x) for x in now) + tuple(from_south(x) for x in now)
-    for q in range(6):
-        fields[q] = outs[q]
+    fields[...] = now
     total = jnp.sum(jnp.sum(square, axis=0, keepdims=True), axis=1, keepdims=True)
-    factor = 1.0 / jnp.sqrt(total * mean + constant)
-    diagonal = lax.broadcasted_iota(jnp.int32, (R * C, S), 0) == lax.broadcasted_iota(
-        jnp.int32, (R * C, S), 1
-    )
-    for q in range(6):
-        row = fields[q, pl.ds(me, 1), :]
-        phase_out[q : q + 1, :] = row * factor
-        only = jnp.where(diagonal, jnp.broadcast_to(row, (R * C, S)), 0.0)
+    factor = 1.0 / jnp.sqrt(total * (1.0 / float(ndev * R * C)) + constant)
+    own = fields[pl.ds(me, 1), :]
+    east_own = fields[pl.ds(jnp.minimum(me + 1, ndev - 1), 1), :]
+    east_own = jnp.where(jnp.full((1, S), last_col), 0.0, east_own)
+    south_own = fields[pl.ds(jnp.minimum(me + nc, ndev - 1), 1), :]
+    south_own = jnp.where(jnp.full((1, S), last_row), 0.0, south_own)
+    phase_out[0:1, :] = own * factor
+    patch = lax.broadcasted_iota(jnp.int32, (R * C, S), 0)
+    ahead = lax.broadcasted_iota(jnp.int32, (R * C, S), 1) - patch
+    inner_j, inner_i = patch % C < C - 1, patch // C < R - 1
+
+    def spread_out(q, only):
         factors[q * R * C : (q + 1) * R * C, :] = (
             jnp.broadcast_to(jnp.sum(only, axis=1, keepdims=True), (R * C, S)) * factor
         )
 
+    for part in range(2):
+        at_part = ahead - part * R * C
+        spread_out(part, jnp.where(at_part == 0, own, 0.0))
+        near = jnp.where(inner_j & (at_part == 1), own, 0.0)
+        spread_out(2 + part, jnp.where(jnp.logical_not(inner_j) & (at_part == 1 - C), east_own, near))
+        near = jnp.where(inner_i & (at_part == C), own, 0.0)
+        spread_out(
+            4 + part, jnp.where(jnp.logical_not(inner_i) & (at_part == -(R - 1) * C), south_own, near)
+        )
+
     all_gathered().wait_send()
 
-    @pl.when(my_col > 0)
-    def _():
-        east_run(0, R, 0, my_col - 1).wait_send()
-
-    for i in range(R - n_relay, R):
-
-        @pl.when(forwards(i))
+    def chunks_sent(n):
+        pltpu.make_async_remote_copy(
+            src_ref=pv.at[pl.ds(0, n * S)],
+            dst_ref=pv.at[pl.ds(0, n * S)],
+            send_sem=e_send.at[0],
+            recv_sem=e_recv.at[0],
+            device_id=others[0],
+            device_id_type=MESH,
+        ).wait_send()
+
+    pair_first = opens & (my_col == nc - 2)
+    pair_last = closes & last_col
+    for n, sender in (
+        (R + n_turn, pair_first),
+        (R + 1, opens & (my_col < nc - 2)),
+        (R + n_relay, pair_last),
+        (R, (my_col > 0) & jnp.logical_not(opens | pair_last)),
+    ):
+
+        @pl.when(sender)
         def _():
-            forward_copy(i, my_col - 2).wait_send()
-
-    for i in range(R - n_turn, R):
-
-        @pl.when(turned_here(i))
-        def _():
-            turn_copy(i, my_col + 1).wait_send()
+            chunks_sent(n)
 
     @pl.when(my_row > 0)
     def _():
@@ -732,11 +748,11 @@
     lax.fori_loop(0, R * C // pair, step, 0)
 
     row8 = lax.broadcasted_iota(jnp.int32, (R, S), 0)
+    line = jnp.broadcast_to(phase[0:1, :], (R, S))
     for part in range(2):
-        line = jnp.broadcast_to(phase[part : part + 1, :], (R, S))
-        plane = line
+        plane = line if part == 0 else pltpu.roll(line, S - R * C, 1)
         for i in range(1, R):
-            plane = jnp.where(row8 == i, pltpu.roll(line, S - i * C, 1), plane)
+            plane = jnp.where(row8 == i, pltpu.roll(line, S - part * R * C - i * C, 1), plane)
         pad[part] = plane[:, :C]
     send = pltpu.make_async_copy(pad, phases, phase_sem.at[0])
     send.start()
@@ -771,9 +787,9 @@
             pltpu.VMEM((2 * PAD + 2 * C * H, S), f32),
             pltpu.VMEM((R * S, S), f32),
             pltpu.VMEM((4 * R * C, S), f32),
-            pltpu.VMEM((3, S), f32),
-            pltpu.VMEM((ndev, 3, S), f32),
-            pltpu.VMEM((6, ndev, S), f32),
+            pltpu.VMEM((3, 1, S), f32),
+            pltpu.VMEM((3, ndev, S), f32),
+            pltpu.VMEM((ndev, S), f32),
             pltpu.SMEM((4, R, C), jnp.int32),
             pltpu.VMEM((n_relays(R) * S, S), f32),
             pltpu.VMEM((min(2, R) * S, S), f32),
@@ -785,8 +801,7 @@
             dma((1,)), dma((1,)),
             dma((1,)),
             pltpu.SemaphoreType.REGULAR((n_rounds(nr) + n_rounds(nc),)),
-            dma((n_relays(R),)), dma((n_relays(R),)),
-            dma((min(2, R),)), dma((min(2, R),)),
+            dma((n_relays(R),)), dma((min(2, R),)),
             pltpu.SemaphoreType.REGULAR((1,)),
         ],
         compiler_params=pltpu.CompilerParams(

time: 26.3 us -> 26.2 us (level)
  no operation moved by 1% of the time
where the time goes in v6:
time: 26.2 us; the launch traced here: 26.1 us
  Pallas kernels  25.4 us (97%)
  between operations  0.64 us (2%)
    pallas_call x1, Pallas kernels, local(): pl.pallas_call(functools.partial(sync_kernel, dims), out_shape=(pltpu.VME...  22 us
    pallas_call x1, Pallas kernels, local(): pl.pallas_call(functools.partial(blend_kernel, (R, C, S, pair)), out_shap...  3.45 us

profile of v6, /device:TPU:0, one launch (start us, length us, event | category | flops | bytes accessed | tf_op | source)
XLA Modules:
  0.0 26.1 jit_solution(6969177219341039011)
XLA Ops:
  0.6 22.0 %sync_patches.1 = (f32[16384,128]{1,0:T(8,128)S(1)}, f32[16384,128]{1,0:T(8,128)S(1)}, f32[9216,128]{1,0:T(8,128)S(1)}, f32[384,128]{1,0:T(8,128)S(1)}, f32[8,128]{1,0:T(8,128)S(1)}) custom-call(f32[16384,128]{1,0:T(8,128)} %bitcast.2, s32[8,8]{1,0:T(8,128)} %ro_in.1, s32[8,8]{1,0:T(8,128)} %rw_in.1, s32[8,8]{1,0:T(8,128)} %do_in.1, s32[8,8]{1,0:T(8,128)} %dw_in.1), custom_call_target="tpu_custom_call" | custom-call | tf_op jit(solution)/shard_map/sync_patches/pallas_call | solution.py:773
  22.6 3.5 %blend_patches.1 = (f32[16384,128]{1,0:T(8,128)}, f32[2,8,8]{2,1,0:T(8,128)}) custom-call(f32[16384,128]{1,0:T(8,128)S(1)} %get-tuple-element.9.aw, f32[16384,128]{1,0:T(8,128)S(1)} %get-tuple-element.10.ew, f32[9216,128]{1,0:T(8,128)S(1)} %get-tuple-element.11.sw, f32[384,128]{1,0:T(8,128)S(1)} %get-tuple-element.12.factors, ...), custom_call_target="tpu_custom_call" | custom-call | tf_op jit(solution)/shard_map/blend_patches/pallas_call | solution.py:813

commit v7 on v6

--- a/solution.py
+++ b/solution.py
@@ -47,7 +47,7 @@
 
 
 def load_groups(n):
-    return groups(n, (1, 1, 2, 4))
+    return groups(n, (1, n))
 
 
 def arrive_groups(n):
@@ -709,7 +709,7 @@
     R, C, S, pair = dims
     lo = S // 2 - 8
     T = S - lo
-    piece = pair * 2 * S
+    piece = pair * 2 * S // 2
 
     def save(k):
         return pltpu.make_async_copy(
@@ -742,7 +742,8 @@
     def step(k, carry):
         for n in range(pair):
             place(k * pair + n)
-        save(k).start()
+        for n in range(2):
+            save(2 * k + n).start()
         return carry
 
     lax.fori_loop(0, R * C // pair, step, 0)

time: 26.2 us -> 26.2 us (level)
  no operation moved by 1% of the time
where the time goes in v7:
time: 26.2 us; the launch traced here: 26 us
  Pallas kernels  25.4 us (97%)
  between operations  0.64 us (2%)
    pallas_call x1, Pallas kernels, local(): pl.pallas_call(functools.partial(sync_kernel, dims), out_shape=(pltpu.VME...  21.9 us
    pallas_call x1, Pallas kernels, local(): pl.pallas_call(functools.partial(blend_kernel, (R, C, S, pair)), out_shap...  3.46 us

profile of v7, /device:TPU:0, one launch (start us, length us, event | category | flops | bytes accessed | tf_op | source)
XLA Modules:
  0.0 26.0 jit_solution(6679587196889103469)
XLA Ops:
  0.6 21.9 %sync_patches.1 = (f32[16384,128]{1,0:T(8,128)S(1)}, f32[16384,128]{1,0:T(8,128)S(1)}, f32[9216,128]{1,0:T(8,128)S(1)}, f32[384,128]{1,0:T(8,128)S(1)}, f32[8,128]{1,0:T(8,128)S(1)}) custom-call(f32[16384,128]{1,0:T(8,128)} %bitcast.2, s32[8,8]{1,0:T(8,128)} %ro_in.1, s32[8,8]{1,0:T(8,128)} %rw_in.1, s32[8,8]{1,0:T(8,128)} %do_in.1, s32[8,8]{1,0:T(8,128)} %dw_in.1), custom_call_target="tpu_custom_call" | custom-call | tf_op jit(solution)/shard_map/sync_patches/pallas_call | solution.py:774
  22.6 3.5 %blend_patches.1 = (f32[16384,128]{1,0:T(8,128)}, f32[2,8,8]{2,1,0:T(8,128)}) custom-call(f32[16384,128]{1,0:T(8,128)S(1)} %get-tuple-element.9.aw, f32[16384,128]{1,0:T(8,128)S(1)} %get-tuple-element.10.ew, f32[9216,128]{1,0:T(8,128)S(1)} %get-tuple-element.11.sw, f32[384,128]{1,0:T(8,128)S(1)} %get-tuple-element.12.factors, ...), custom_call_target="tpu_custom_call" | custom-call | tf_op jit(solution)/shard_map/blend_patches/pallas_call | solution.py:814
